TPU v7x, 32 devices: a whole 2x2x4 slice. The times are simulated.
32 devices in a mesh: row: 16 (over z, y, core), col: 2 (over x).
Axes of the slice: x: 2, y: 2, z: 4, core: 2. Of those that a mesh axis runs over, the one named last changes fastest.
Arguments:
- x_in: bfloat16 [2, 16384, 768], P(None, 'row', 'col'), may hold values from -6 to 6
- span_start: int32 [2, 16, 2], P(None, 'row'), may hold values from 0 to 768, as said below
- span_kind: int32 [2, 16, 2], P(None, 'row'), may hold values from 0 to 1
- ln1_gain: float32 [768], P('col'), may hold values from 0.5 to 1.5
- ln1_bias: float32 [768], P('col'), may hold values from -3 to 3
- w_qkv: bfloat16 [768, 3, 768], P('row', None, 'col'), may hold values from -0.3125 to 0.3125
- b_query: float32 [768], P('col'), may hold values from -3 to 3
- b_value: float32 [768], P('col'), may hold values from -3 to 3
- w_out: bfloat16 [768, 768], P('col', 'row'), may hold values from -0.875 to 0.875
- b_out: float32 [768], P('col'), may hold values from -3 to 3
- ln2_gain: float32 [768], P('col'), may hold values from 0.5 to 1.5
- ln2_bias: float32 [768], P('col'), may hold values from -3 to 3
- w_fc: bfloat16 [768, 3072], P('row', 'col'), may hold values from -0.21875 to 0.21875
- b_fc: float32 [3072], P('col'), may hold values from -3 to 3
- w_proj: bfloat16 [3072, 768], P('col', 'row'), may hold values from -0.15625 to 0.15625
- b_proj: float32 [768], P('col'), may hold values from -3 to 3
- cotangent: bfloat16 [2, 16384, 768], P(None, 'row', 'col'), may hold values from -6 to 6
Outputs:
- layer_out: bfloat16 [2, 16384, 768], P(None, 'row', 'col')
- grad_input: bfloat16 [2, 16384, 768], P(None, 'row', 'col')
- g_ln1_gain: float32 [768], P('col')
- g_ln1_bias: float32 [768], P('col')
- g_w_qkv: float32 [768, 3, 768], P('row', None, 'col')
- g_b_query: float32 [768], P('col')
- g_b_value: float32 [768], P('col')
- g_w_out: float32 [768, 768], P('col', 'row')
- g_b_out: float32 [768], P('col')
- g_ln2_gain: float32 [768], P('col')
- g_ln2_bias: float32 [768], P('col')
- g_w_fc: float32 [768, 3072], P('row', 'col')
- g_b_fc: float32 [3072], P('col')
- g_w_proj: float32 [3072, 768], P('col', 'row')
- g_b_proj: float32 [768], P('col')
Inputs may be any that keep to these rules, and one draw needn't show every extreme that they name: `span_start`: span j of a sequence starts within the j-th of 2 equal parts of the sequence and ends within it, so spans never intersect.
All inputs are finite; a program needn't handle non-finite values.
Results may differ from a plain program's by a relative error of at most 0.017.
Values may be sent and summed in bfloat16 or wider, within the bound.
A program may use at most 192 MiB of HBM per device.

v0:
```python
from functools import partial

import jax
import jax.numpy as jnp
from jax import lax
from jax.sharding import PartitionSpec as P

HEAD = 64
IMG = 256


epsilon = 1e-05


def contract_rows(left, right):
    return lax.dot_general(
        left, right, (((0,), (0,)), ((), ())), preferred_element_type=jnp.float32
    )


def contract_cols(left, right):
    return lax.dot_general(
        left, right, (((1,), (1,)), ((), ())), preferred_element_type=jnp.float32
    )


def fetch_blocks(w_qkv, w_out, w_fc, w_proj):
    return (
        lax.all_gather(w_qkv, "row", axis=0, tiled=True),
        lax.all_gather(w_out, "row", axis=1, tiled=True),
        lax.all_gather(w_fc, "row", axis=0, tiled=True),
        lax.all_gather(w_proj, "row", axis=1, tiled=True),
    )


def reduce_blocks(grad_qkv, grad_out, grad_fc, grad_proj):
    return (
        lax.psum_scatter(grad_qkv, "row", scatter_dimension=0, tiled=True),
        lax.psum_scatter(grad_out, "row", scatter_dimension=1, tiled=True),
        lax.psum_scatter(grad_fc, "row", scatter_dimension=0, tiled=True),
        lax.psum_scatter(grad_proj, "row", scatter_dimension=1, tiled=True),
    )


def norm_forward(residual, gain, bias):
    model_width = residual.shape[-1] * lax.axis_size("col")
    first_sum, second_sum = lax.psum(
        (jnp.sum(residual, axis=-1), jnp.sum(residual * residual, axis=-1)), "col"
    )
    average = first_sum / model_width
    inverse = lax.rsqrt(second_sum / model_width - average * average + epsilon)
    centred = (residual - average[:, None]) * inverse[:, None]
    normed = (centred * gain + bias).astype(jnp.bfloat16)
    return (lax.all_gather(normed, "col", axis=1, tiled=True), centred, inverse)


def norm_backward(grad_half, centred, inverse, gain):
    model_width = grad_half.shape[-1] * lax.axis_size("col")
    scaled = grad_half * gain
    first_sum, second_sum = lax.psum(
        (jnp.sum(scaled, axis=-1), jnp.sum(scaled * centred, axis=-1)), "col"
    )
    back = inverse[:, None] * (
        scaled - first_sum[:, None] / model_width - centred * second_sum[:, None] / model_width
    )
    return (back, jnp.sum(grad_half * centred, axis=0), jnp.sum(grad_half, axis=0))


def branch_sum(partial_out):
    return lax.psum_scatter(
        partial_out.astype(jnp.bfloat16), "col", scatter_dimension=1, tiled=True
    ).astype(jnp.float32)


def input_sum(partial_in):
    return lax.psum_scatter(
        partial_in.astype(jnp.bfloat16), "col", scatter_dimension=1, tiled=True
    ).astype(jnp.float32)


def spread_grad(grad_half):
    return lax.all_gather(grad_half, "col", axis=1, tiled=True)


def span_allowed(query_pos, length, starts, span_types):
    columns = jnp.arange(length, dtype=jnp.int32)
    causal = columns[None, :] <= query_pos[:, None]
    inside_query = (query_pos[:, None] >= starts[None, :]) & (
        query_pos[:, None] < starts[None, :] + IMG
    )
    inside_key = (columns[:, None] >= starts[None, :]) & (columns[:, None] < starts[None, :] + IMG)
    joined = inside_query[:, None, :] & inside_key[None, :, :] & (span_types[None, None, :] == 1)
    return causal | jnp.any(joined, axis=-1)


def attend_forward(query, key_rows, values, starts, span_types):
    length = query.shape[0]
    block_rows = min(512, length)

    def one_block(first_row):
        query_pos = first_row + jnp.arange(block_rows, dtype=jnp.int32)
        query_block = lax.dynamic_slice_in_dim(query, first_row, block_rows, 0)
        scores = (
            jnp.einsum("qhd,khd->hqk", query_block, key_rows, preferred_element_type=jnp.float32)
            * 0.125
        )
        scores = jnp.where(span_allowed(query_pos, length, starts, span_types)[None], scores, -1e30)
        largest = jnp.max(scores, axis=-1, keepdims=True)
        weights = jnp.exp(scores - largest)
        totals = jnp.sum(weights, axis=-1, keepdims=True)
        chance = (weights / totals).astype(jnp.bfloat16)
        attended = jnp.einsum("hqk,khd->qhd", chance, values, preferred_element_type=jnp.float32)
        return (attended.astype(jnp.bfloat16), (largest + jnp.log(totals))[:, :, 0])

    first_rows = jnp.arange(length // block_rows, dtype=jnp.int32) * block_rows
    attended, log_total = lax.map(one_block, first_rows)
    return (attended.reshape(query.shape), log_total)


def attend_backward(query, key_rows, values, log_total, grad_attended, starts, span_types):
    length = query.shape[0]
    block_rows = min(512, length)

    def one_block(running, block_item):
        first_row, log_block = block_item
        query_pos = first_row + jnp.arange(block_rows, dtype=jnp.int32)
        query_block = lax.dynamic_slice_in_dim(query, first_row, block_rows, 0)
        grad_block = lax.dynamic_slice_in_dim(grad_attended, first_row, block_rows, 0)
        scores = (
            jnp.einsum("qhd,khd->hqk", query_block, key_rows, preferred_element_type=jnp.float32)
            * 0.125
        )
        scores = jnp.where(span_allowed(query_pos, length, starts, span_types)[None], scores, -1e30)
        chance = jnp.exp(scores - log_block[:, :, None])
        grad_chance = jnp.einsum(
            "qhd,khd->hqk", grad_block, values, preferred_element_type=jnp.float32
        )
        rowdot = jnp.sum(chance * grad_chance, axis=-1, keepdims=True)
        grad_scores = (chance * (grad_chance - rowdot) * 0.125).astype(jnp.bfloat16)
        grad_query = jnp.einsum(
            "hqk,khd->qhd", grad_scores, key_rows, preferred_element_type=jnp.float32
        )
        grad_keys = running[0] + jnp.einsum(
            "hqk,qhd->khd", grad_scores, query_block, preferred_element_type=jnp.float32
        )
        grad_values = running[1] + jnp.einsum(
            "hqk,qhd->khd",
            chance.astype(jnp.bfloat16),
            grad_block,
            preferred_element_type=jnp.float32,
        )
        return ((grad_keys, grad_values), grad_query)

    empty = jnp.zeros(key_rows.shape, jnp.float32)
    first_rows = jnp.arange(length // block_rows, dtype=jnp.int32) * block_rows
    (grad_keys, grad_values), grad_query = lax.scan(
        one_block, (empty, empty), (first_rows, log_total)
    )
    return (grad_query.reshape(query.shape), grad_keys, grad_values)


def body(
    x_in,
    span_start,
    span_kind,
    ln1_gain,
    ln1_bias,
    w_qkv,
    b_query,
    b_value,
    w_out,
    b_out,
    ln2_gain,
    ln2_bias,
    w_fc,
    b_fc,
    w_proj,
    b_proj,
    cotangent,
):
    micro_count, tok_rows, half_width = x_in.shape
    model_width = half_width * lax.axis_size("col")
    heads_here = half_width // HEAD
    seq_count = span_start.shape[1]
    length = tok_rows // seq_count
    large_total = None
    small_total = None
    outputs = []
    grads_in = []
    for micro_step in range(micro_count):
        gathered = fetch_blocks(w_qkv, w_out, w_fc, w_proj)
        qkv_w, out_w, fc_w, proj_w = gathered
        residual = x_in[micro_step].astype(jnp.float32)
        starts = span_start[micro_step]
        span_types = span_kind[micro_step]
        qkv_flat = qkv_w.reshape(model_width, 3 * half_width)
        normed_first, centred_first, inverse_first = norm_forward(residual, ln1_gain, ln1_bias)
        packed = jnp.dot(normed_first, qkv_flat, preferred_element_type=jnp.float32).reshape(
            tok_rows, 3, half_width
        )
        bias_rows = jnp.stack([b_query, jnp.zeros_like(b_query), b_value])
        packed = (packed + bias_rows[None]).astype(jnp.bfloat16)
        heads_view = packed.reshape(seq_count, length, 3, heads_here, HEAD)

        def seq_forward(seq_item):
            piece_view, seq_starts, seq_types = seq_item
            return attend_forward(
                piece_view[:, 0], piece_view[:, 1], piece_view[:, 2], seq_starts, seq_types
            )

        attended, log_total = lax.map(seq_forward, (heads_view, starts, span_types))
        attended = attended.reshape(tok_rows, half_width)
        middle = (
            residual
            + branch_sum(jnp.dot(attended, out_w, preferred_element_type=jnp.float32))
            + b_out
        )
        normed_second, centred_second, inverse_second = norm_forward(middle, ln2_gain, ln2_bias)
        hidden = jnp.dot(normed_second, fc_w, preferred_element_type=jnp.float32) + b_fc
        active_full, gelu_back = jax.vjp(partial(jax.nn.gelu, approximate=True), hidden)
        active = active_full.astype(jnp.bfloat16)
        result = (
            middle
            + branch_sum(jnp.dot(active, proj_w, preferred_element_type=jnp.float32))
            + b_proj
        )
        outputs.append(result.astype(jnp.bfloat16))
        gathered = fetch_blocks(w_qkv, w_out, w_fc, w_proj)
        qkv_w, out_w, fc_w, proj_w = gathered
        qkv_flat = qkv_w.reshape(model_width, 3 * half_width)
        grad_out = cotangent[micro_step]
        grad_full = spread_grad(grad_out)
        grad_proj = contract_rows(active, grad_full)
        grad_active = contract_cols(grad_full, proj_w)
        grad_hidden = gelu_back(grad_active)[0].astype(jnp.bfloat16)
        grad_fc = contract_rows(normed_second, grad_hidden)
        grad_bfc = jnp.sum(grad_hidden.astype(jnp.float32), axis=0)
        grad_normed_second = input_sum(contract_cols(grad_hidden, fc_w))
        back_second, grad_gain_second, grad_bias_second = norm_backward(
            grad_normed_second, centred_second, inverse_second, ln2_gain
        )
        grad_out_wide = grad_out.astype(jnp.float32)
        grad_middle = grad_out_wide + back_second
        grad_bproj = jnp.sum(grad_out_wide, axis=0)
        grad_bout = jnp.sum(grad_middle, axis=0)
        grad_middle_full = spread_grad(grad_middle.astype(jnp.bfloat16))
        grad_outw = contract_rows(attended, grad_middle_full)
        grad_attended = contract_cols(grad_middle_full, out_w).astype(jnp.bfloat16)
        grad_attended = grad_attended.reshape(seq_count, length, heads_here, HEAD)

        def seq_backward(seq_item):
            piece_view, seq_log, seq_grad, seq_starts, seq_types = seq_item
            return attend_backward(
                piece_view[:, 0],
                piece_view[:, 1],
                piece_view[:, 2],
                seq_log,
                seq_grad,
                seq_starts,
                seq_types,
            )

        grad_query, grad_keys, grad_values = lax.map(
            seq_backward, (heads_view, log_total, grad_attended, starts, span_types)
        )
        grad_packed = (
            jnp.stack([grad_query, grad_keys, grad_values], axis=2)
            .reshape(tok_rows, 3, half_width)
            .astype(jnp.bfloat16)
        )
        grad_bquery = jnp.sum(grad_packed[:, 0].astype(jnp.float32), axis=0)
        grad_bvalue = jnp.sum(grad_packed[:, 2].astype(jnp.float32), axis=0)
        flat_grads = grad_packed.reshape(tok_rows, 3 * half_width)
        grad_qkv = contract_rows(normed_first, flat_grads).reshape(model_width, 3, half_width)
        grad_normed_first = input_sum(contract_cols(flat_grads, qkv_flat))
        back_first, grad_gain_first, grad_bias_first = norm_backward(
            grad_normed_first, centred_first, inverse_first, ln1_gain
        )
        grads_in.append((grad_middle + back_first).astype(jnp.bfloat16))
        large_now = (grad_qkv, grad_outw, grad_fc, grad_proj)
        large_now = reduce_blocks(grad_qkv, grad_outw, grad_fc, grad_proj)
        if large_total is None:
            large_total = large_now
        else:
            large_total = tuple((earlier + added for earlier, added in zip(large_total, large_now)))
        small_now = (
            grad_gain_first,
            grad_bias_first,
            grad_bquery,
            grad_bvalue,
            grad_bout,
            grad_gain_second,
            grad_bias_second,
            grad_bfc,
            grad_bproj,
        )
        if small_total is None:
            small_total = small_now
        else:
            small_total = tuple((earlier + added for earlier, added in zip(small_total, small_now)))
    small_total = lax.psum(
        (
            small_total[0],
            small_total[1],
            small_total[2],
            small_total[3],
            small_total[4],
            small_total[5],
            small_total[6],
            small_total[7],
            small_total[8],
        ),
        "row",
    )
    return (
        jnp.stack(outputs),
        jnp.stack(grads_in),
        small_total[0],
        small_total[1],
        large_total[0],
        small_total[2],
        small_total[3],
        large_total[1],
        small_total[4],
        small_total[5],
        small_total[6],
        large_total[2],
        small_total[7],
        large_total[3],
        small_total[8],
    )


def solution(mesh):
    placed = (
        P(None, "row", "col"),
        P(None, "row", None),
        P(None, "row", None),
        P("col"),
        P("col"),
        P("row", None, "col"),
        P("col"),
        P("col"),
        P("col", "row"),
        P("col"),
        P("col"),
        P("col"),
        P("row", "col"),
        P("col"),
        P("col", "row"),
        P("col"),
        P(None, "row", "col"),
    )
    return jax.shard_map(
        body,
        mesh=mesh,
        in_specs=placed,
        out_specs=(
            P(None, "row", "col"),
            P(None, "row", "col"),
            P("col"),
            P("col"),
            P("row", None, "col"),
            P("col"),
            P("col"),
            P("col", "row"),
            P("col"),
            P("col"),
            P("col"),
            P("row", "col"),
            P("col"),
            P("col", "row"),
            P("col"),
        ),
        check_vma=False,
    )
```

profile of v0, /device:TPU:0, one launch (start us, length us, event | category | flops | bytes accessed | tf_op | source)
XLA Modules:
  0.0 1278.4 jit_solution(7627922101752689925)
XLA Ops:
  22.5 25.8 %all_gather.50 = bf16[384,768]{0,1:T(8,128)(2,1)} all-gather(bf16[384,48]{0,1:T(8,128)(2,1)S(1)} %copy-done.61), channel_id=1, replica_groups=mesh['row'=16,'col'=2] {'row'}, dimensions={1}, use_global_device_ids=true | all-gather | bytes 626688 | tf_op jit(solution)/shard_map/all_gather | solution.py:30
  86.4 32.0 %while.95 = (s32[]{:T(128)}, bf16[2,512,6,64]{1,3,2,0:T(8,128)(2,1)S(1)}, f32[2,6,512]{2,1,0:T(8,128)}, s32[2]{0:T(128)S(1)}, s32[2]{0:T(128)S(1)}, /*index=5*/s...) while((s32[]{:T(128)}, ...), condition=%wide.region_23.24_spmd, body=%wide.region_19.23_spmd.sunk | while | flops 846928384 | bytes 43376884 | solution.py:116
  131.1 32.0 %while.94 = (s32[]{:T(128)}, bf16[2,512,6,64]{1,3,2,0:T(8,128)(2,1)S(1)}, f32[2,6,512]{2,1,0:T(8,128)}, s32[2]{0:T(128)S(1)}, s32[2]{0:T(128)S(1)}, /*index=5*/s...) while((s32[]{:T(128)}, ...), condition=%wide.region_8.9_spmd, body=%wide.region_4.8_spmd.sunk | while | flops 846928384 | bytes 43376884 | solution.py:116
  212.6 27.9 %all-gather.20.cloned.1.call-done = bf16[768,1536]{1,0:T(8,128)(2,1)} async-done(((bf16[48,1536]{1,0:T(8,128)(2,1)}), bf16[768,1536]{1,0:T(8,128)(2,1)}) %all-gather.20.cloned.1.call-update) | async-done | bytes 2359312 | tf_op jit(solution)/shard_map/all_gather | solution.py:31
  240.6 28.0 %all-gather.26.cloned.1.call-done = bf16[1024,768]{1,0:T(8,128)(2,1)} async-done(((bf16[1024,384]{1,0:T(8,128)(2,1)}), bf16[1024,768]{1,0:T(8,128)(2,1)}) %all-gather.26.cloned.1.call-update) | async-done | bytes 1572880 | tf_op jit(solution)/shard_map/all_gather | solution.py:54
  276.0 37.2 %all-gather.22.cloned.1.call-done = bf16[1536,768]{0,1:T(8,128)(2,1)} async-done(((bf16[1536,48]{0,1:T(8,128)(2,1)}), bf16[1536,768]{0,1:T(8,128)(2,1)}) %all-gather.22.cloned.1.call-update) | async-done | bytes 2359312 | tf_op jit(solution)/shard_map/all_gather | solution.py:32
  429.2 26.1 %reduce-scatter.49.cloned.1.call-done = bf16[384,1024]{1,0:T(8,128)(2,1)} async-done(((bf16[768,1024]{1,0:T(8,128)(2,1)}), bf16[384,1024]{1,0:T(8,128)(2,1)}) %reduce-scatter.49.cloned.1.call-update) | async-done | bytes 786448
  457.7 26.0 %reduce-scatter.39.cloned.1.call-done = bf16[384,1024]{1,0:T(8,128)(2,1)} async-done(((bf16[768,1024]{1,0:T(8,128)(2,1)}), bf16[384,1024]{1,0:T(8,128)(2,1)}) %reduce-scatter.39.cloned.1.call-update) | async-done | bytes 786448
  486.0 26.5 %reduce-scatter.45.cloned.1.call-done = bf16[384,1024]{1,0:T(8,128)(2,1)} async-done(((bf16[768,1024]{1,0:T(8,128)(2,1)}), bf16[384,1024]{1,0:T(8,128)(2,1)}) %reduce-scatter.45.cloned.1.call-update) | async-done | bytes 786448
  535.8 27.3 %all-gather.30.cloned.1.call-done = bf16[1024,768]{1,0:T(8,128)(2,1)} async-done(((bf16[1024,384]{1,0:T(8,128)(2,1)}), bf16[1024,768]{1,0:T(8,128)(2,1)}) %all-gather.30.cloned.1.call-update) | async-done | bytes 1572880 | tf_op jit(solution)/shard_map/all_gather | solution.py:82
  567.7 179.1 %while.97 = (s32[]{:T(128)}, f32[1024,6,64]{0,2,1:T(8,128)}, f32[1024,6,64]{0,2,1:T(8,128)}, bf16[2,512,6,64]{1,0,3,2:T(2,128)(2,1)}, s32[2]{0:T(128)S(1)}, /*in...) while((s32[]{:T(128)}, f32[1024,6,64]{0,2,1:T(8,128)}, ...), condition=%wide.region_52.53_spmd.clone, body=%wide.region_49.52_spmd.clone.sunk | while | flops 2100315648 | bytes 195264912 | solution.py:156
  587.0 25.9 %fusion.374 = bf16[1,512,6,64]{1,3,2,0:T(8,128)(2,1)S(1)} fusion(bf16[1024,6,64]{0,2,1:T(8,128)(2,1)S(1)} %get-tuple-element.1027, f32[6,512,1024]{2,1,0:T(8,128)} %fusion.371, f32[6,512,1024]{2,1,0:T(8,128)} %copy-done, f32[6,512]{1,0:T(8,128)S(1)} %dynamic-slice_bitcast_fusion.5, pred[512,1024]{1,0:T(8,128)(4,1)S(1)} %fusion.373), kind=kOutput, calls=%fused_computation.117.clone.1 | convolution fusion | flops 437260288 | bytes 26882048 | tf_op jit(solution)/shard_map/while/body/eval_jaxpr/while/body/eval_jaxpr/hqk,khd->qhd/dot_general | solution.py:140
  613.0 29.4 %bitcast_add_fusion.10 = f32[1024,6,64]{0,2,1:T(8,128)} fusion(f32[1024,6,64]{0,2,1:T(8,128)} %get-tuple-element.1005, f32[6,512,1024]{2,1,0:T(8,128)} %fusion.371, f32[6,512,1024]{2,1,0:T(8,128)} %copy-done, f32[6,512]{1,0:T(8,128)S(1)} %dynamic-slice_bitcast_fusion.5, pred[512,1024]{1,0:T(8,128)(4,1)S(1)} %fusion.373, pred[]{:T(512)S(6)} %compare.7, ...), kind=kOutput, calls=%fused_computation.116.clone.1 | convolution fusion | flops 438046720 | bytes 54951940 | tf_op jit(solution)/shard_map/while/body/eval_jaxpr/while/body/eval_jaxpr/hqk,qhd->khd/dot_general | solution.py:143
  676.2 25.9 %fusion.374 = bf16[1,512,6,64]{1,3,2,0:T(8,128)(2,1)S(1)} fusion(bf16[1024,6,64]{0,2,1:T(8,128)(2,1)S(1)} %get-tuple-element.1027, f32[6,512,1024]{2,1,0:T(8,128)} %fusion.371, f32[6,512,1024]{2,1,0:T(8,128)} %copy-done, f32[6,512]{1,0:T(8,128)S(1)} %dynamic-slice_bitcast_fusion.5, pred[512,1024]{1,0:T(8,128)(4,1)S(1)} %fusion.373), kind=kOutput, calls=%fused_computation.117.clone.1 | convolution fusion | flops 437260288 | bytes 26882048 | tf_op jit(solution)/shard_map/while/body/eval_jaxpr/while/body/eval_jaxpr/hqk,khd->qhd/dot_general | solution.py:140
  702.1 29.7 %bitcast_add_fusion.10 = f32[1024,6,64]{0,2,1:T(8,128)} fusion(f32[1024,6,64]{0,2,1:T(8,128)} %get-tuple-element.1005, f32[6,512,1024]{2,1,0:T(8,128)} %fusion.371, f32[6,512,1024]{2,1,0:T(8,128)} %copy-done, f32[6,512]{1,0:T(8,128)S(1)} %dynamic-slice_bitcast_fusion.5, pred[512,1024]{1,0:T(8,128)(4,1)S(1)} %fusion.373, pred[]{:T(512)S(6)} %compare.7, ...), kind=kOutput, calls=%fused_computation.116.clone.1 | convolution fusion | flops 438046720 | bytes 54951940 | tf_op jit(solution)/shard_map/while/body/eval_jaxpr/while/body/eval_jaxpr/hqk,qhd->khd/dot_general | solution.py:143
  762.7 179.3 %while.96 = (s32[]{:T(128)}, f32[1024,6,64]{0,2,1:T(8,128)}, f32[1024,6,64]{0,2,1:T(8,128)}, bf16[2,512,6,64]{1,0,3,2:T(2,128)(2,1)}, s32[2]{0:T(128)S(1)}, /*in...) while((s32[]{:T(128)}, f32[1024,6,64]{0,2,1:T(8,128)}, ...), condition=%wide.region_38.39_spmd.clone, body=%wide.region_35.38_spmd.clone.sunk | while | flops 2100315648 | bytes 195264912 | solution.py:156
  782.1 26.0 %fusion.360 = bf16[1,512,6,64]{1,3,2,0:T(8,128)(2,1)S(1)} fusion(bf16[1024,6,64]{0,2,1:T(8,128)(2,1)S(1)} %get-tuple-element.982, f32[6,512,1024]{2,1,0:T(8,128)} %fusion.357, f32[6,512,1024]{2,1,0:T(8,128)} %copy-done.1, f32[6,512]{1,0:T(8,128)S(1)} %dynamic-slice_bitcast_fusion.4, pred[512,1024]{1,0:T(8,128)(4,1)S(1)} %fusion.359), kind=kOutput, calls=%fused_computation.69.clone.1 | convolution fusion | flops 437260288 | bytes 26882048 | tf_op jit(solution)/shard_map/while/body/eval_jaxpr/while/body/eval_jaxpr/hqk,khd->qhd/dot_general | solution.py:140
  808.1 29.3 %bitcast_add_fusion.8 = f32[1024,6,64]{0,2,1:T(8,128)} fusion(f32[1024,6,64]{0,2,1:T(8,128)} %get-tuple-element.960, f32[6,512,1024]{2,1,0:T(8,128)} %fusion.357, f32[6,512,1024]{2,1,0:T(8,128)} %copy-done.1, f32[6,512]{1,0:T(8,128)S(1)} %dynamic-slice_bitcast_fusion.4, pred[512,1024]{1,0:T(8,128)(4,1)S(1)} %fusion.359, pred[]{:T(512)S(6)} %compare.6, ...), kind=kOutput, calls=%fused_computation.68.clone.1 | convolution fusion | flops 438046720 | bytes 54951940 | tf_op jit(solution)/shard_map/while/body/eval_jaxpr/while/body/eval_jaxpr/hqk,qhd->khd/dot_general | solution.py:143
  871.3 25.9 %fusion.360 = bf16[1,512,6,64]{1,3,2,0:T(8,128)(2,1)S(1)} fusion(bf16[1024,6,64]{0,2,1:T(8,128)(2,1)S(1)} %get-tuple-element.982, f32[6,512,1024]{2,1,0:T(8,128)} %fusion.357, f32[6,512,1024]{2,1,0:T(8,128)} %copy-done.1, f32[6,512]{1,0:T(8,128)S(1)} %dynamic-slice_bitcast_fusion.4, pred[512,1024]{1,0:T(8,128)(4,1)S(1)} %fusion.359), kind=kOutput, calls=%fused_computation.69.clone.1 | convolution fusion | flops 437260288 | bytes 26882048 | tf_op jit(solution)/shard_map/while/body/eval_jaxpr/while/body/eval_jaxpr/hqk,khd->qhd/dot_general | solution.py:140
  897.2 29.6 %bitcast_add_fusion.8 = f32[1024,6,64]{0,2,1:T(8,128)} fusion(f32[1024,6,64]{0,2,1:T(8,128)} %get-tuple-element.960, f32[6,512,1024]{2,1,0:T(8,128)} %fusion.357, f32[6,512,1024]{2,1,0:T(8,128)} %copy-done.1, f32[6,512]{1,0:T(8,128)S(1)} %dynamic-slice_bitcast_fusion.4, pred[512,1024]{1,0:T(8,128)(4,1)S(1)} %fusion.359, pred[]{:T(512)S(6)} %compare.6, ...), kind=kOutput, calls=%fused_computation.68.clone.1 | convolution fusion | flops 438046720 | bytes 54951940 | tf_op jit(solution)/shard_map/while/body/eval_jaxpr/while/body/eval_jaxpr/hqk,qhd->khd/dot_general | solution.py:143
  1012.4 60.9 %all-reduce = (f32[384]{0:T(512)}, f32[384]{0:T(512)}, f32[384]{0:T(512)}, f32[384]{0:T(512)}, f32[384]{0:T(512)}, /*index=5*/f32[384]{0:T(512)}, f32[384]{0:T(512)}, f32[1536]{0:T(1024)}, f32[384]{0:T(512)}) all-reduce(f32[384]{0:T(512)S(1)} %add.441, f32[384]{0:T(512)S(1)} %add.442, ...), channel_id=1, replica_groups=mesh['row'=16,'col'=2] {'row'}, use_global_device_ids=true, to_apply=%region_60.61 | all-reduce | flops 4608 | bytes 36864 | tf_op jit(solution)/shard_map/psum | solution.py:301
  1084.9 35.6 %reduce-scatter.35.cloned.1.call-done = f32[1536,48]{0,1:T(8,128)} async-done(((f32[1536,768]{0,1:T(8,128)}), f32[1536,48]{0,1:T(8,128)}) %reduce-scatter.35.cloned.1.call-update) | async-done | bytes 294928 | tf_op jit(solution)/shard_map/reduce_scatter | solution.py:41
  1120.6 79.3 %reduce-scatter.33.cloned.1.call-done = f32[48,1536]{1,0:T(8,128)} async-done(((f32[768,1536]{1,0:T(8,128)}), f32[48,1536]{1,0:T(8,128)}) %reduce-scatter.33.cloned.1.call-update) | async-done | bytes 294928 | tf_op jit(solution)/shard_map/reduce_scatter | solution.py:40
  1199.8 71.8 %reduce-scatter.29.cloned.1.call-done = f32[48,3,384]{2,0,1:T(8,128)} async-done(((f32[768,3,384]{2,0,1:T(8,128)}), f32[48,3,384]{2,0,1:T(8,128)}) %reduce-scatter.29.cloned.1.call-update) | async-done | bytes 221200 | tf_op jit(solution)/shard_map/reduce_scatter | solution.py:38
  (483 shorter events, 551.2 us)
Async XLA Ops:
  7.2 46.8 %all-gather.16.cloned.1.call-start = ((), (), s32[]{:S(2)}) async-start(), calls=%async_computation.13 | async-start | bytes 1880064 | tf_op jit(solution)/shard_map/all_gather | solution.py:29
  7.9 74.1 %all-gather.24.cloned.1.call-start = ((), (), s32[]{:S(2)}) async-start(), calls=%async_computation.17 | async-start | bytes 2359296 | tf_op jit(solution)/shard_map/all_gather | solution.py:54
  21.6 96.8 %all-gather.14.cloned.1.call-start = ((), (), s32[]{:S(2)}) async-start(), calls=%async_computation.12 | async-start | bytes 2359296 | tf_op jit(solution)/shard_map/all_gather | solution.py:54
  22.4 148.0 %reduce-scatter.41.cloned.1.call-start = ((), (), s32[]{:S(2)}) async-start(), calls=%async_computation.29 | async-start | bytes 2359296
  130.3 65.7 %reduce-scatter.37.cloned.1.call-start = ((), (), s32[]{:S(2)}) async-start(), calls=%async_computation.27 | async-start | bytes 2359296
  169.8 70.8 %all-gather.20.cloned.1.call-start = ((), (), s32[]{:S(2)}) async-start(), calls=%async_computation.15 | async-start | bytes 2506752 | tf_op jit(solution)/shard_map/all_gather | solution.py:31
  170.4 98.3 %all-gather.26.cloned.1.call-start = ((), (), s32[]{:S(2)}) async-start(), calls=%async_computation.18 | async-start | bytes 2359296 | tf_op jit(solution)/shard_map/all_gather | solution.py:54
  207.5 105.7 %all-gather.22.cloned.1.call-start = ((), (), s32[]{:S(2)}) async-start(), calls=%async_computation.16 | async-start | bytes 2506752 | tf_op jit(solution)/shard_map/all_gather | solution.py:32
  208.3 132.5 %all-gather.34.cloned.1.call-start = ((), (), s32[]{:S(2)}) async-start(), calls=%async_computation.22 | async-start | bytes 2359296 | tf_op jit(solution)/shard_map/all_gather | solution.py:82
  211.0 158.9 %all-gather.18.cloned.1.call-start = ((), (), s32[]{:S(2)}) async-start(), calls=%async_computation.14 | async-start | bytes 2359296 | tf_op jit(solution)/shard_map/all_gather | solution.py:54
  211.6 187.1 %all-gather.32.cloned.1.call-start = ((), (), s32[]{:S(2)}) async-start(), calls=%async_computation.21 | async-start | bytes 2359296 | tf_op jit(solution)/shard_map/all_gather | solution.py:82
  212.4 100.9 %copy-start.91 = (f32[1536]{0:T(1024)S(1)}, f32[1536]{0:T(1024)}, u32[]{:S(2)}) copy-start(f32[1536]{0:T(1024)} %param.38) | copy-start | bytes 18436
  212.4 214.6 %reduce-scatter.43.cloned.1.call-start = ((), (), s32[]{:S(2)}) async-start(), calls=%async_computation.30 | async-start | bytes 2359296
  324.5 130.8 %reduce-scatter.49.cloned.1.call-start = ((), (), s32[]{:S(2)}) async-start(), calls=%async_computation.33 | async-start | bytes 2359296
  358.2 125.5 %reduce-scatter.39.cloned.1.call-start = ((), (), s32[]{:S(2)}) async-start(), calls=%async_computation.28 | async-start | bytes 2359296
  385.2 127.3 %reduce-scatter.45.cloned.1.call-start = ((), (), s32[]{:S(2)}) async-start(), calls=%async_computation.31 | async-start | bytes 2359296
  416.2 146.9 %all-gather.30.cloned.1.call-start = ((), (), s32[]{:S(2)}) async-start(), calls=%async_computation.20 | async-start | bytes 2359296 | tf_op jit(solution)/shard_map/all_gather | solution.py:82
  534.6 223.4 %all-gather.28.cloned.1.call-start = ((), (), s32[]{:S(2)}) async-start(), calls=%async_computation.19 | async-start | bytes 2359296 | tf_op jit(solution)/shard_map/all_gather | solution.py:82
  535.7 468.7 %reduce-scatter.51.cloned.1.call-start = ((), (), s32[]{:S(2)}) async-start(), calls=%async_computation.34 | async-start | bytes 2359296
  757.9 249.0 %reduce-scatter.47.cloned.1.call-start = ((), (), s32[]{:S(2)}) async-start(), calls=%async_computation.32 | async-start | bytes 2359296
  953.0 132.0 %reduce-scatter.31.cloned.1.call-start = ((), (), s32[]{:S(2)}) async-start(), calls=%async_computation.24 | async-start | bytes 1253376 | tf_op jit(solution)/shard_map/reduce_scatter | solution.py:39
  957.8 162.8 %reduce-scatter.35.cloned.1.call-start = ((), (), s32[]{:S(2)}) async-start(), calls=%async_computation.26 | async-start | bytes 5013504 | tf_op jit(solution)/shard_map/reduce_scatter | solution.py:41
  973.1 226.7 %reduce-scatter.33.cloned.1.call-start = ((), (), s32[]{:S(2)}) async-start(), calls=%async_computation.25 | async-start | bytes 5013504 | tf_op jit(solution)/shard_map/reduce_scatter | solution.py:40
  983.9 287.8 %reduce-scatter.29.cloned.1.call-start = ((), (), s32[]{:S(2)}) async-start(), calls=%async_computation.23 | async-start | bytes 3760128 | tf_op jit(solution)/shard_map/reduce_scatter | solution.py:38
  (103 other events, 755.9 us)
Sparse Core Ops, SparseCore 0:
  10.3 43.6 all-gather.15
  56.2 25.8 all-gather.23
  84.2 27.1 all-gather.13
  130.5 26.1 reduce-scatter.40
  169.9 26.1 reduce-scatter.36
  198.2 42.3 all-gather.19
  242.7 25.8 all-gather.25
  270.9 42.3 all-gather.21
  314.8 25.8 all-gather.33
  342.7 27.1 all-gather.17
  371.5 27.1 all-gather.31
  400.8 26.1 reduce-scatter.42
  429.2 26.1 reduce-scatter.48
  457.5 26.1 reduce-scatter.38
  486.3 26.1 reduce-scatter.44
  534.7 28.3 all-gather.29
  564.5 27.2 all-gather.27
  757.9 26.1 reduce-scatter.50
  953.1 26.1 reduce-scatter.46
  983.3 58.2 reduce-scatter.30
  1046.0 74.5 reduce-scatter.34
  1125.0 74.7 reduce-scatter.32
  1204.3 67.3 reduce-scatter.28
where the time goes:
time: 1300 us; the launch traced here: 1280 us
  waiting for transfers between devices  497 us (38%)
  matrix products  413 us (32%)
  local copies, waits for them, and re-layouts  155 us (12%)
  blocking collectives  117 us (9%)
  other arithmetic  62 us (5%)
  loops' own time  17.4 us (1%)
  between operations  15.5 us (1%)
    dot_general x4, matrix products, one_block(): jnp.einsum('hqk,qhd->khd', grad_scores, query_block, preferred_element_ty...  118 us
    unnamed x31, waiting for transfers between devices  118 us
    dot_general x4, matrix products, one_block(): jnp.einsum('hqk,khd->qhd', grad_scores, key_rows, preferred_element_type=...  104 us
    reduce_scatter x1, waiting for transfers between devices, reduce_blocks(): lax.psum_scatter(grad_fc, 'row', scatter_dimension=0, tiled=True)  79.3 us
    reduce_scatter x1, waiting for transfers between devices, reduce_blocks(): lax.psum_scatter(grad_qkv, 'row', scatter_dimension=0, tiled=True)  71.8 us
    all_gather x4, waiting for transfers between devices, norm_forward(): return (lax.all_gather(normed, 'col', axis=1, tiled=True), centred, inverse)  64.7 us
    psum x1, blocking collectives, body(): lax.psum((small_total[0], small_total[1], small_total[2], small_total[3],...  60.9 us
    dynamic_update_slice x8, local copies, waits for them, and re-layouts, attend_backward(): lax.scan(one_block, (empty, empty), (first_rows, log_total))  58.7 us
  transfers between devices with their start and end apart: 23, of which 17 were waited for; matrix products, arithmetic and copies ran while one was open for 45% of the time, Pallas kernels for 0%

commit v1 on v0

v1 whole, which is shorter than its diff:
```python
import jax
import jax.numpy as jnp
from jax import lax
from jax.experimental import pallas as pl
from jax.experimental.pallas import tpu as pltpu
from jax.sharding import PartitionSpec as P

HEAD = 64
IMG = 256
epsilon = 1e-05
bf16 = jnp.bfloat16
f32 = jnp.float32
GELU_A = 0.7978845608028654
GELU_B = 0.044715
PAIR = 2 * HEAD


def nn(a, b):
    return lax.dot_general(a, b, (((1,), (0,)), ((), ())), preferred_element_type=f32)


def nt(a, b):
    return lax.dot_general(a, b, (((1,), (1,)), ((), ())), preferred_element_type=f32)


def tn(a, b):
    return lax.dot_general(a, b, (((0,), (0,)), ((), ())), preferred_element_type=f32)


def half_bias(span_ref, part, half):
    start = span_ref[0, part]
    kind = span_ref[1, part]
    base = part * half
    rows = lax.broadcasted_iota(jnp.int32, (half, half), 0) + base
    cols = lax.broadcasted_iota(jnp.int32, (half, half), 1) + base
    first = jnp.where(kind == 1, start, 4 * half)
    joined = (rows >= first) & (rows < first + IMG) & (cols >= first) & (cols < first + IMG)
    return jnp.where((cols <= rows) | joined, 0.0, -1e30).astype(f32)


def lane_masks(rows):
    lane = lax.broadcasted_iota(jnp.int32, (rows, PAIR), 1)
    return lane < HEAD


def attend_forward_kernel(span_ref, q_ref, k_ref, v_ref, o_ref, p_ref, inv_ref, bias_ref):
    half = q_ref.shape[0] // 2

    @pl.when(pl.program_id(0) == 0)
    def _():
        for part in range(2):
            bias_ref[part] = half_bias(span_ref, part, half)

    low = lane_masks(half)
    for part in range(2):
        q = q_ref[part * half : (part + 1) * half, :] * jnp.asarray(0.125, bf16)
        zero = jnp.zeros_like(q)
        outs = []
        invs = []
        for head in range(2):
            mine = low if head == 0 else jnp.logical_not(low)
            qh = jnp.where(mine, q, zero)
            own = nt(qh, k_ref[part * half : (part + 1) * half, :]) + bias_ref[part]
            largest = jnp.max(own, axis=1, keepdims=True)
            if part == 1:
                before = nt(qh, k_ref[:half, :])
                largest = jnp.maximum(largest, jnp.max(before, axis=1, keepdims=True))
            own = jnp.exp(own - largest)
            total = jnp.sum(own, axis=1, keepdims=True)
            own = own.astype(bf16)
            p_ref[0, head, 2 * part] = own
            out = nn(own, v_ref[part * half : (part + 1) * half, :])
            if part == 1:
                before = jnp.exp(before - largest)
                total = total + jnp.sum(before, axis=1, keepdims=True)
                before = before.astype(bf16)
                p_ref[0, head, 1] = before
                out = out + nn(before, v_ref[:half, :])
            inv = 1.0 / total
            outs.append(out * inv)
            invs.append(inv)
        o_ref[part * half : (part + 1) * half, :] = jnp.where(low, outs[0], outs[1]).astype(bf16)
        inv_ref[part * half : (part + 1) * half, :] = jnp.where(low, invs[0], invs[1])


def qkv_specs(length, half_blocks):
    def spec(which):
        return pl.BlockSpec(
            (length, PAIR),
            lambda j: (0, (j // half_blocks) * 3 * half_blocks + which * half_blocks + j % half_blocks),
        )

    return [spec(0), spec(1), spec(2)]


def attend_forward(packed, spans):
    length = packed.shape[0]
    width = packed.shape[1] // 3
    pairs = width // PAIR
    half = length // 2
    return pl.pallas_call(
        attend_forward_kernel,
        grid=(pairs,),
        in_specs=[pl.BlockSpec(memory_space=pltpu.SMEM)] + qkv_specs(length, pairs // 2),
        out_specs=[
            pl.BlockSpec((length, PAIR), lambda j: (0, j)),
            pl.BlockSpec((1, 2, 3, half, half), lambda j: (j, 0, 0, 0, 0)),
            pl.BlockSpec((length, PAIR), lambda j: (0, j)),
        ],
        out_shape=[
            jax.ShapeDtypeStruct((length, width), bf16),
            jax.ShapeDtypeStruct((pairs, 2, 3, half, half), bf16),
            jax.ShapeDtypeStruct((length, width), f32),
        ],
        scratch_shapes=[pltpu.VMEM((2, half, half), f32)],
        compiler_params=pltpu.CompilerParams(vmem_limit_bytes=60 << 20),
        cost_estimate=pl.CostEstimate(
            flops=4 * 3 * half * half * width * 4, bytes_accessed=24 << 20, transcendentals=3 * half * half * 12
        ),
        name="attend_forward",
    )(spans, packed, packed, packed)


def attend_backward_kernel(q_ref, k_ref, v_ref, o_ref, p_ref, inv_ref, g_ref, dq_ref, dk_ref, dv_ref):
    half = q_ref.shape[0] // 2
    low = lane_masks(half)
    dks = [None, None]
    dvs = [None, None]

    def add(total, part, value):
        total[part] = value if total[part] is None else total[part] + value

    for part in range(2):
        rows = slice(part * half, (part + 1) * half)
        inv = inv_ref[rows, :]
        g = g_ref[rows, :].astype(f32) * inv
        scaled = g * o_ref[rows, :].astype(f32)
        q = q_ref[rows, :]
        gb = g.astype(bf16)
        zero = jnp.zeros_like(gb)
        dq = None
        for head in range(2):
            mine = low if head == 0 else jnp.logical_not(low)
            gh = jnp.where(mine, gb, zero)
            qh = jnp.where(mine, q, zero)
            rowdot = jnp.sum(jnp.where(mine, scaled, 0.0), axis=1, keepdims=True)
            for kpart in range(part + 1):
                krows = slice(kpart * half, (kpart + 1) * half)
                p = p_ref[0, head, part + kpart]
                kh = jnp.where(mine, k_ref[krows, :], zero)
                dp = nt(gh, v_ref[krows, :])
                ds = (p.astype(f32) * (dp - rowdot)).astype(bf16)
                term = nn(ds, kh)
                dq = term if dq is None else dq + term
                add(dks, kpart, tn(ds, qh))
                add(dvs, kpart, tn(p, gh))
        dq_ref[rows, :] = (dq * 0.125).astype(bf16)
    for part in range(2):
        rows = slice(part * half, (part + 1) * half)
        dk_ref[rows, :] = (dks[part] * 0.125).astype(bf16)
        dv_ref[rows, :] = dvs[part].astype(bf16)


def attend_backward(packed, attended, p, inv, grad_attended):
    length = packed.shape[0]
    width = packed.shape[1] // 3
    pairs = width // PAIR
    half = length // 2
    one = pl.BlockSpec((length, PAIR), lambda j: (0, j))
    return pl.pallas_call(
        attend_backward_kernel,
        grid=(pairs,),
        in_specs=qkv_specs(length, pairs // 2)
        + [one, pl.BlockSpec((1, 2, 3, half, half), lambda j: (j, 0, 0, 0, 0)), one, one],
        out_specs=[one, one, one],
        out_shape=[jax.ShapeDtypeStruct((length, width), bf16)] * 3,
        compiler_params=pltpu.CompilerParams(vmem_limit_bytes=60 << 20),
        cost_estimate=pl.CostEstimate(
            flops=8 * 3 * half * half * width * 4, bytes_accessed=32 << 20, transcendentals=0
        ),
        name="attend_backward",
    )(packed, packed, packed, attended, p, inv, grad_attended)


SWAP = [(0, 1), (1, 0)]


def swap(value):
    return lax.ppermute(value, "col", SWAP)


def ordered(mine, other, axis):
    first = lax.axis_index("col") == 0
    low = jnp.where(first, mine, other)
    high = jnp.where(first, other, mine)
    return jnp.concatenate([low, high], axis=axis)


def own_micro(halves):
    col = lax.axis_index("col")
    mine = lax.dynamic_index_in_dim(halves, col, 0, keepdims=False)
    other = swap(lax.dynamic_index_in_dim(halves, 1 - col, 0, keepdims=False))
    return ordered(mine, other, 1)


def back_micro(full):
    col = lax.axis_index("col")
    half = full.shape[1] // 2
    mine = lax.dynamic_slice_in_dim(full, col * half, half, 1)
    other = swap(lax.dynamic_slice_in_dim(full, (1 - col) * half, half, 1))
    first = col == 0
    return jnp.stack([jnp.where(first, mine, other), jnp.where(first, other, mine)])


def gather_weights(block):
    return lax.all_gather(block, ("col", "row"), axis=0, tiled=True)


def scatter_grad(total):
    return lax.psum_scatter(total, ("col", "row"), scatter_dimension=0, tiled=True)


def layer_norm(value):
    width = value.shape[-1]
    average = jnp.sum(value, axis=-1, keepdims=True) / width
    square = jnp.sum(value * value, axis=-1, keepdims=True) / width
    inverse = lax.rsqrt(square - average * average + epsilon)
    return (value - average) * inverse, inverse


def norm_backward(grad, centred, inverse, gain):
    scaled = grad * gain
    first = jnp.mean(scaled, axis=-1, keepdims=True)
    second = jnp.mean(scaled * centred, axis=-1, keepdims=True)
    back = inverse * (scaled - first - centred * second)
    return back, jnp.sum(grad * centred, axis=0), jnp.sum(grad, axis=0)


def body(
    x_in, span_start, span_kind, ln1_gain, ln1_bias, w_qkv, b_query, b_value, w_out, b_out,
    ln2_gain, ln2_bias, w_fc, b_fc, w_proj, b_proj, cotangent,
):
    half_width = x_in.shape[2]
    width = 2 * half_width
    ff_half = w_fc.shape[1]
    shard = w_qkv.shape[0]
    col = lax.axis_index("col")

    qkv_all = gather_weights(w_qkv.reshape(shard, 3 * half_width)).reshape(2, width, 3 * half_width)
    residual = own_micro(x_in).astype(f32)
    out_all = gather_weights(w_out.T).reshape(2, width, half_width)
    fc_all = gather_weights(w_fc).reshape(2, width, ff_half)
    proj_all = gather_weights(w_proj.T).reshape(2, width, ff_half)
    grad_out = own_micro(cotangent)

    vectors = [ln1_gain, ln1_bias, b_query, b_value, b_out, ln2_gain, ln2_bias, b_fc, b_proj]
    flat = jnp.concatenate(vectors)
    flat_other = swap(flat)
    full = []
    at = 0
    for vector in vectors:
        full.append(ordered(vector, flat_other[at : at + vector.shape[0]], 0))
        at += vector.shape[0]
    ln1_gain, ln1_bias, b_query, b_value, b_out, ln2_gain, ln2_bias, b_fc, b_proj = full

    starts = lax.dynamic_index_in_dim(span_start, col, 0, keepdims=False)[0]
    kinds = lax.dynamic_index_in_dim(span_kind, col, 0, keepdims=False)[0]
    spans = jnp.stack([starts, kinds])

    centred_first, inverse_first = layer_norm(residual)
    normed_first = (centred_first * ln1_gain + ln1_bias).astype(bf16)
    zero = jnp.zeros((half_width,), f32)
    pieces = []
    for h in range(2):
        part = slice(h * half_width, (h + 1) * half_width)
        bias = jnp.concatenate([b_query[part], zero, b_value[part]])
        pieces.append((nn(normed_first, qkv_all[h]) + bias).astype(bf16))
    packed = jnp.concatenate(pieces, axis=1)
    attended, p, inv = attend_forward(packed, spans)
    branch = nt(attended[:, :half_width], out_all[0]) + nt(attended[:, half_width:], out_all[1])
    middle = residual + branch + b_out
    centred_second, inverse_second = layer_norm(middle)
    normed_second = (centred_second * ln2_gain + ln2_bias).astype(bf16)
    branch = None
    slopes = []
    actives = []
    for h in range(2):
        hidden = nn(normed_second, fc_all[h]) + b_fc[h * ff_half : (h + 1) * ff_half]
        squared = hidden * hidden
        tanh = jnp.tanh(GELU_A * hidden * (1.0 + GELU_B * squared))
        active = (0.5 * hidden * (1.0 + tanh)).astype(bf16)
        slope = 0.5 * (1.0 + tanh) + 0.5 * hidden * (1.0 - tanh * tanh) * GELU_A * (
            1.0 + 3.0 * GELU_B * squared
        )
        slopes.append(slope.astype(bf16))
        actives.append(active)
        term = nt(active, proj_all[h])
        branch = term if branch is None else branch + term
    layer_out = back_micro((middle + branch + b_proj).astype(bf16))

    grad_out_wide = grad_out.astype(f32)
    g_proj = [tn(grad_out, active).astype(bf16) for active in actives]
    grad_hidden = [(nn(grad_out, proj_all[h]) * slopes[h].astype(f32)).astype(bf16) for h in range(2)]
    g_fc = [tn(normed_second, grad) for grad in grad_hidden]
    g_bfc = jnp.concatenate([jnp.sum(grad.astype(f32), axis=0) for grad in grad_hidden])
    out_proj = scatter_grad(jnp.concatenate([g.astype(bf16) for g in g_proj], axis=0))
    out_fc = scatter_grad(jnp.concatenate([g.astype(bf16) for g in g_fc], axis=0))
    grad_normed = nt(grad_hidden[0], fc_all[0]) + nt(grad_hidden[1], fc_all[1])
    back, g_ln2_gain, g_ln2_bias = norm_backward(grad_normed, centred_second, inverse_second, ln2_gain)
    grad_middle = grad_out_wide + back
    g_bproj = jnp.sum(grad_out_wide, axis=0)
    g_bout = jnp.sum(grad_middle, axis=0)
    grad_low = grad_middle.astype(bf16)
    g_out = [tn(grad_low, attended[:, h * half_width : (h + 1) * half_width]) for h in range(2)]
    out_out = scatter_grad(jnp.concatenate([g.astype(bf16) for g in g_out], axis=0))
    grad_attended = jnp.concatenate([nn(grad_low, out_all[h]).astype(bf16) for h in range(2)], axis=1)
    dq, dk, dv = attend_backward(packed, attended, p, inv, grad_attended)
    g_bquery = jnp.sum(dq.astype(f32), axis=0)
    g_bvalue = jnp.sum(dv.astype(f32), axis=0)
    grad_packed = []
    for h in range(2):
        part = slice(h * half_width, (h + 1) * half_width)
        grad_packed.append(jnp.concatenate([dq[:, part], dk[:, part], dv[:, part]], axis=1))
    g_qkv = [tn(normed_first, grad) for grad in grad_packed]
    out_qkv = scatter_grad(jnp.concatenate([g.astype(bf16) for g in g_qkv], axis=0))
    grad_normed = nt(grad_packed[0], qkv_all[0]) + nt(grad_packed[1], qkv_all[1])
    back, g_ln1_gain, g_ln1_bias = norm_backward(grad_normed, centred_first, inverse_first, ln1_gain)
    grad_input = back_micro((grad_middle + back).astype(bf16))

    small = [g_ln1_gain, g_ln1_bias, g_bquery, g_bvalue, g_bout, g_ln2_gain, g_ln2_bias, g_bfc, g_bproj]
    summed = lax.psum(jnp.concatenate(small), ("row", "col"))
    kept = []
    at = 0
    for vector in small:
        size = vector.shape[0] // 2
        kept.append(lax.dynamic_slice_in_dim(summed, at + col * size, size, 0))
        at += vector.shape[0]
    return (
        layer_out,
        grad_input,
        kept[0],
        kept[1],
        out_qkv.astype(f32).reshape(shard, 3, half_width),
        kept[2],
        kept[3],
        out_out.astype(f32).T,
        kept[4],
        kept[5],
        kept[6],
        out_fc.astype(f32),
        kept[7],
        out_proj.astype(f32).T,
        kept[8],
    )


def solution(mesh):
    placed = (
        P(None, "row", "col"), P(None, "row", None), P(None, "row", None), P("col"), P("col"),
        P("row", None, "col"), P("col"), P("col"), P("col", "row"), P("col"), P("col"), P("col"),
        P("row", "col"), P("col"), P("col", "row"), P("col"), P(None, "row", "col"),
    )
    return jax.shard_map(
        body,
        mesh=mesh,
        in_specs=placed,
        out_specs=(
            P(None, "row", "col"), P(None, "row", "col"), P("col"), P("col"), P("row", None, "col"),
            P("col"), P("col"), P("col", "row"), P("col"), P("col"), P("col"), P("row", "col"),
            P("col"), P("col", "row"), P("col"),
        ),
        check_vma=False,
    )
```

time: 1300 us -> 742 us (0.57); the launches traced: 1280 us -> 735 us
  matrix products: 413 us -> 96.1 us
  local copies, waits for them, and re-layouts: 155 us -> 28.2 us
  blocking collectives: 117 us -> 58.5 us
  waiting for transfers between devices: 497 us -> 446 us
  Pallas kernels: 0 us -> 48.7 us
  other arithmetic: 62 us -> 34.1 us
  loops' own time: 17.4 us -> 0 us
    dot_general x52 -> x24, matrix products: 413 us -> 96.1 us  [the longest x8 38.8 us: nn(): lax.dot_general(a, b, (((1,), (0,)), ((), ())), preferred_element_type=f32)]
    unnamed x31 -> x8, waiting for transfers between devices: 118 us -> 1.98 us
    reduce_scatter x4, waiting for transfers between devices: 187 us -> 262 us  [scatter_grad(): lax.psum_scatter(total, ('col', 'row'), scatter_dimension=0, tiled=True)]
    dynamic_update_slice x8 -> x0, local copies, waits for them, and re-layouts: 58.7 us -> none  [attend_backward(): lax.scan(one_block, (empty, empty), (first_rows, log_total))]
    pallas_call x0 -> x2, Pallas kernels: none -> 48.7 us  [the longest x1 27.2 us: attend_backward(): pl.pallas_call(attend_backward_kernel, grid=(pairs,), in_specs=qkv_specs(...]
    all_gather x11 -> x4, waiting for transfers between devices: 192 us -> 147 us  [gather_weights(): return lax.all_gather(block, ('col', 'row'), axis=0, tiled=True)]
    unnamed x194 -> x149, local copies, waits for them, and re-layouts: 52.9 us -> 14.8 us
    ppermute x0 -> x5, waiting for transfers between devices: none -> 35.9 us  [swap(): return lax.ppermute(value, 'col', SWAP)]
  transfers between devices with their start and end apart: 23 -> 13, of which waited for: 17 -> 9; matrix products, arithmetic and copies ran while one was open for 45% -> 16% of each run, Pallas kernels for 0% -> 7%
where the time goes in v1:
time: 742 us; the launch traced here: 735 us
  waiting for transfers between devices  446 us (60%)
  matrix products  96.1 us (13%)
  blocking collectives  58.5 us (8%)
  Pallas kernels  48.7 us (7%)
  other arithmetic  34.1 us (5%)
  local copies, waits for them, and re-layouts  28.2 us (4%)
  between operations  15.8 us (2%)
  starting transfers between devices  7.61 us (1%)
    reduce_scatter x4, waiting for transfers between devices, scatter_grad(): lax.psum_scatter(total, ('col', 'row'), scatter_dimension=0, tiled=True)  262 us
    all_gather x4, waiting for transfers between devices, gather_weights(): return lax.all_gather(block, ('col', 'row'), axis=0, tiled=True)  147 us
    psum x1, blocking collectives, body(): summed = lax.psum(jnp.concatenate(small), ('row', 'col'))  58.5 us
    dot_general x8, matrix products, nn(): lax.dot_general(a, b, (((1,), (0,)), ((), ())), preferred_element_type=f32)  38.8 us
    ppermute x5, waiting for transfers between devices, swap(): return lax.ppermute(value, 'col', SWAP)  35.9 us
    dot_general x8, matrix products, nt(): lax.dot_general(a, b, (((1,), (1,)), ((), ())), preferred_element_type=f32)  30.5 us
    pallas_call x1, Pallas kernels, attend_backward(): pl.pallas_call(attend_backward_kernel, grid=(pairs,), in_specs=qkv_specs(...  27.2 us
    dot_general x8, matrix products, tn(): lax.dot_general(a, b, (((0,), (0,)), ((), ())), preferred_element_type=f32)  26.9 us
  transfers between devices with their start and end apart: 13, of which 9 were waited for; matrix products, arithmetic and copies ran while one was open for 16% of the time, Pallas kernels for 7%

profile of v1, /device:TPU:0, one launch (start us, length us, event | category | flops | bytes accessed | tf_op | source)
XLA Modules:
  0.0 735.3 jit_solution(3533910975484032872)
XLA Ops:
  28.7 18.3 %collective-permute-done = bf16[1024,384]{0,1:T(8,128)(2,1)} collective-permute-done((bf16[1024,384]{0,1:T(8,128)(2,1)}, bf16[1024,384]{0,1:T(8,128)(2,1)}, u32[]{:S(2)}, u32[]{:S(2)}) %collective-permute-start) | collective-permute-done | bytes 786464 | tf_op jit(solution)/shard_map/ppermute | solution.py:189
  48.8 17.5 %collective-permute-done.3 = bf16[1024,384]{0,1:T(8,128)(2,1)} collective-permute-done((bf16[1024,384]{0,1:T(8,128)(2,1)}, bf16[1024,384]{0,1:T(8,128)(2,1)}, u32[]{:S(2)}, u32[]{:S(2)}) %collective-permute-start.3) | collective-permute-done | bytes 786464 | tf_op jit(solution)/shard_map/ppermute | solution.py:189
  68.7 9.7 %all-gather.5.cloned.1.call-done = bf16[1536,1152]{1,0:T(8,128)(2,1)} async-done(((bf16[48,1152]{1,0:T(8,128)(2,1)}), bf16[1536,1152]{1,0:T(8,128)(2,1)}) %all-gather.5.cloned.1.call-update) | async-done | bytes 3538960 | tf_op jit(solution)/shard_map/all_gather | solution.py:216
  78.4 4.1 add_convert_fusion.2
  87.4 21.5 %attend_forward.1 = (bf16[1024,768]{1,0:T(8,128)(2,1)}, bf16[6,2,3,512,512]{4,3,2,1,0:T(8,128)(2,1)}, f32[1024,768]{1,0:T(8,128)}) custom-call(s32[2,2]{1,0:T(2,128)} %pad_add_fusion.span_ref, bf16[1024,2304]{1,0:T(8,128)(2,1)} %pad_maximum_fusion.q_ref.k_ref.v_ref, bf16[1024,2304]{1,0:T(8,128)(2,1)} %pad_maximum_fusion.q_ref.k_ref.v_ref, ...), custom_call_target="tpu_custom_call" | custom-call | flops 9663676416 | bytes 25165824 | tf_op jit(solution)/shard_map/attend_forward/pallas_call | solution.py:101
  108.9 25.0 %all-gather.7.cloned.1.call-done = bf16[1536,384]{1,0:T(8,128)(2,1)} async-done(((bf16[48,384]{1,0:T(8,128)(2,1)}), bf16[1536,384]{1,0:T(8,128)(2,1)}) %all-gather.7.cloned.1.call-update) | async-done | bytes 1179664 | tf_op jit(solution)/shard_map/all_gather | solution.py:216
  139.8 59.5 %all-gather.9.cloned.1.call-done = bf16[1536,1536]{1,0:T(8,128)(2,1)} async-done(((bf16[48,1536]{1,0:T(8,128)(2,1)}), bf16[1536,1536]{1,0:T(8,128)(2,1)}) %all-gather.9.cloned.1.call-update) | async-done | bytes 4718608 | tf_op jit(solution)/shard_map/all_gather | solution.py:216
  199.3 7.6 %fusion.20 = f32[1024,1536]{1,0:T(8,128)} fusion(bf16[1024,768]{0,1:T(8,128)(2,1)} %add_convert_fusion.5, bf16[1536,1536]{1,0:T(8,128)(2,1)} %all-gather.9.cloned.1.call-done), kind=kOutput, calls=%fused_computation.60 | convolution fusion | flops 2415919104 | bytes 10223616 | tf_op jit(solution)/shard_map/dot_general | solution.py:19
  207.0 4.6 fusion.27
  211.6 52.4 %all-gather.11.cloned.1.call-done = bf16[1536,1536]{1,0:T(8,128)(2,1)} async-done(((bf16[48,1536]{1,0:T(8,128)(2,1)}), bf16[1536,1536]{1,0:T(8,128)(2,1)}) %all-gather.11.cloned.1.call-update) | async-done | bytes 4718608 | tf_op jit(solution)/shard_map/all_gather | solution.py:216
  264.0 9.7 %convert_reduce_fusion = (f32[1536]{0:T(1024)S(1)}, bf16[1024,1536]{1,0:T(8,128)(2,1)S(1)}) fusion(f32[1024,1536]{1,0:T(8,128)} %fusion.20, f32[1536]{0:T(1024)S(1)} %get-tuple-element.99, bf16[1536,1536]{1,0:T(8,128)(2,1)} %all-gather.11.cloned.1.call-done, bf16[1024,384]{0,1:T(8,128)(2,1)} %get-tuple-element.83, bf16[1024,384]{0,1:T(8,128)(2,1)} %get-tuple-element.82), kind=kOutput, calls=%fused_computation | convolution fusion | flops 2455239168 | bytes 13381632 | tf_op jit(solution)/shard_map/dot_general | solution.py:19
  273.8 5.5 fusion.18
  280.2 6.5 convert_reduce_fusion.1
  290.2 3.9 fusion.70
  303.8 27.2 %attend_backward.1 = (bf16[1024,768]{1,0:T(8,128)(2,1)}, bf16[1024,768]{1,0:T(8,128)(2,1)}, bf16[1024,768]{1,0:T(8,128)(2,1)}) custom-call(bf16[1024,2304]{1,0:T(8,128)(2,1)} %pad_maximum_fusion.q_ref.k_ref.v_ref, bf16[1024,2304]{1,0:T(8,128)(2,1)} %pad_maximum_fusion.q_ref.k_ref.v_ref, bf16[1024,2304]{1,0:T(8,128)(2,1)} %pad_maximum_fusion.q_ref.k_ref.v_ref, ...), custom_call_target="tpu_custom_call" | custom-call | flops 19327352832 | bytes 33554432 | tf_op jit(solution)/shard_map/attend_backward/pallas_call | solution.py:170
  343.0 6.3 convolution_convert_fusion
  349.3 5.6 convolution_convert_fusion.1
  358.1 5.1 convolution_convert_fusion.2
  368.9 5.9 fusion.16
  374.8 6.7 add_convert_fusion.4
  393.3 58.5 %psum.7 = f32[9216]{0:T(1024)S(1)} all-reduce(f32[9216]{0:T(1024)S(1)} %constant_dynamic-update-slice_fusion.13), channel_id=1, replica_groups=mesh['row'=16,'col'=2] {'row','col'}, use_global_device_ids=true, to_apply=%region_18.19 | all-reduce | flops 9216 | bytes 73728 | tf_op jit(solution)/shard_map/psum | solution.py:331
  461.1 41.0 %reduce-scatter.5.cloned.1.call-done = bf16[48,1152]{1,0:T(8,128)(2,1)} async-done(((bf16[1536,1152]{1,0:T(8,128)(2,1)}), bf16[48,1152]{1,0:T(8,128)(2,1)}) %reduce-scatter.5.cloned.1.call-update) | async-done | bytes 110608 | tf_op jit(solution)/shard_map/reduce_scatter | solution.py:220
  503.7 110.5 %reduce-scatter.11.cloned.1.call-done = bf16[48,1536]{1,0:T(8,128)(2,1)} async-done(((bf16[1536,1536]{1,0:T(8,128)(2,1)}), bf16[48,1536]{1,0:T(8,128)(2,1)}) %reduce-scatter.11.cloned.1.call-update) | async-done | bytes 147472 | tf_op jit(solution)/shard_map/reduce_scatter | solution.py:220
  615.9 110.4 %reduce-scatter.9.cloned.1.call-done = bf16[48,1536]{1,0:T(8,128)(2,1)} async-done(((bf16[1536,1536]{1,0:T(8,128)(2,1)}), bf16[48,1536]{1,0:T(8,128)(2,1)}) %reduce-scatter.9.cloned.1.call-update) | async-done | bytes 147472 | tf_op jit(solution)/shard_map/reduce_scatter | solution.py:220
  (245 shorter events, 96.4 us)
Async XLA Ops:
  7.2 71.2 %all-gather.5.cloned.1.call-start = ((), (), s32[]{:S(2)}) async-start(), calls=%async_computation.4 | async-start | bytes 3649536 | tf_op jit(solution)/shard_map/all_gather | solution.py:216
  8.8 125.1 %all-gather.7.cloned.1.call-start = ((), (), s32[]{:S(2)}) async-start(), calls=%async_computation.5 | async-start | bytes 1216512 | tf_op jit(solution)/shard_map/all_gather | solution.py:216
  9.6 189.8 %all-gather.9.cloned.1.call-start = ((), (), s32[]{:S(2)}) async-start(), calls=%async_computation.6 | async-start | bytes 4866048 | tf_op jit(solution)/shard_map/all_gather | solution.py:216
  10.3 253.7 %all-gather.11.cloned.1.call-start = ((), (), s32[]{:S(2)}) async-start(), calls=%async_computation.7 | async-start | bytes 4866048 | tf_op jit(solution)/shard_map/all_gather | solution.py:216
  10.9 448.9 %reduce-scatter.7.cloned.1.call-start = ((), (), s32[]{:S(2)}) async-start(), calls=%async_computation.9 | async-start | bytes 1216512 | tf_op jit(solution)/shard_map/reduce_scatter | solution.py:220
  17.1 10.8 %collective-permute-start.1 = (f32[4608]{0:T(1024)S(1)}, f32[4608]{0:T(1024)S(1)}, u32[]{:S(2)}, u32[]{:S(2)}) collective-permute-start(f32[4608]{0:T(1024)S(1)} %constant_dynamic-update-slice_fusion.8), channel_id=1, source_target_pairs={{0,1},{1,0},{2,3},{3,2},{4,5},{5,4},{6,7},{7,6},{8,9},{9,8},{10,11... | collective-permute-start | bytes 55304 | tf_op jit(solution)/shard_map/ppermute | solution.py:189
  23.6 23.5 %collective-permute-start = (bf16[1024,384]{0,1:T(8,128)(2,1)}, bf16[1024,384]{0,1:T(8,128)(2,1)}, u32[]{:S(2)}, u32[]{:S(2)}) collective-permute-start(bf16[1024,384]{0,1:T(8,128)(2,1)} %bitcast.45), channel_id=1, source_target_pairs={{0,1},{1,0},{2,3},{3,2},{4,5},{5,4},{6,7},{7,6},{8,9},{9,8},{10,11... | collective-permute-start | bytes 2359304 | tf_op jit(solution)/shard_map/ppermute | solution.py:189
  24.8 41.5 %collective-permute-start.3 = (bf16[1024,384]{0,1:T(8,128)(2,1)}, bf16[1024,384]{0,1:T(8,128)(2,1)}, u32[]{:S(2)}, u32[]{:S(2)}) collective-permute-start(bf16[1024,384]{0,1:T(8,128)(2,1)} %bitcast.9), channel_id=1, source_target_pairs={{0,1},{1,0},{2,3},{3,2},{4,5},{5,4},{6,7},{7,6},{8,9},{9,8},{10,11... | collective-permute-start | bytes 2359304 | tf_op jit(solution)/shard_map/ppermute | solution.py:189
  48.3 34.2 %copy-start.2 = (bf16[1024,384]{0,1:T(8,128)(2,1)}, bf16[1024,384]{0,1:T(8,128)(2,1)S(1)}, u32[]{:S(2)}) copy-start(bf16[1024,384]{0,1:T(8,128)(2,1)S(1)} %get-tuple-element.86) | copy-start | bytes 2359300
  48.3 34.2 %copy-start.6 = (bf16[1024,384]{0,1:T(8,128)(2,1)}, bf16[1024,384]{0,1:T(8,128)(2,1)S(1)}, u32[]{:S(2)}) copy-start(bf16[1024,384]{0,1:T(8,128)(2,1)S(1)} %get-tuple-element.87) | copy-start | bytes 2359300
  137.8 148.9 %copy-start = (f32[1024,768]{0,1:T(8,128)}, f32[1024,768]{0,1:T(8,128)S(1)}, u32[]{:S(2)}) copy-start(f32[1024,768]{0,1:T(8,128)S(1)} %get-tuple-element.134) | copy-start | bytes 9437188
  199.3 7.6 %copy-start.22 = (bf16[1024,768]{0,1:T(8,128)(2,1)S(1)}, bf16[1024,768]{0,1:T(8,128)(2,1)}, u32[]{:S(2)}) copy-start(bf16[1024,768]{0,1:T(8,128)(2,1)} %add_convert_fusion.5) | copy-start | bytes 4718596
  199.3 7.6 %copy-start.56 = (bf16[1536,1536]{1,0:T(8,128)(2,1)S(1)}, bf16[1536,1536]{1,0:T(8,128)(2,1)}, u32[]{:S(2)}) copy-start(bf16[1536,1536]{1,0:T(8,128)(2,1)} %all-gather.9.cloned.1.call-done) | copy-start | bytes 14155780
  273.8 13.0 %slice-start = ((s8[4718592]{0:T(1024)(128)(4,1)}), s8[4194304]{0:T(1024)(128)(4,1)S(1)}, s32[]{:S(2)}) async-start(s8[4718592]{0:T(1024)(128)(4,1)} %bitcast.51), calls=%async_computation.12 | async-start | bytes 8388608
  298.7 203.4 %reduce-scatter.5.cloned.1.call-start = ((), (), s32[]{:S(2)}) async-start(), calls=%async_computation.8 | async-start | bytes 3649536 | tf_op jit(solution)/shard_map/reduce_scatter | solution.py:220
  342.7 271.6 %reduce-scatter.11.cloned.1.call-start = ((), (), s32[]{:S(2)}) async-start(), calls=%async_computation.11 | async-start | bytes 4866048 | tf_op jit(solution)/shard_map/reduce_scatter | solution.py:220
  357.4 368.9 %reduce-scatter.9.cloned.1.call-start = ((), (), s32[]{:S(2)}) async-start(), calls=%async_computation.10 | async-start | bytes 4866048 | tf_op jit(solution)/shard_map/reduce_scatter | solution.py:220
  374.8 9.3 %copy-start.33 = (bf16[1024,384]{1,0:T(8,128)(2,1)S(1)}, bf16[1024,384]{1,0:T(8,128)(2,1)}, u32[]{:S(2)}) copy-start(bf16[1024,384]{1,0:T(8,128)(2,1)} %copy-done.32) | copy-start | bytes 2359300
  374.8 9.3 %copy-start.35 = (bf16[1024,384]{1,0:T(8,128)(2,1)S(1)}, bf16[1024,384]{1,0:T(8,128)(2,1)}, u32[]{:S(2)}) copy-start(bf16[1024,384]{1,0:T(8,128)(2,1)} %copy-done.34) | copy-start | bytes 2359300
  374.8 9.3 %copy-start.37 = (bf16[1024,384]{1,0:T(8,128)(2,1)S(1)}, bf16[1024,384]{1,0:T(8,128)(2,1)}, u32[]{:S(2)}) copy-start(bf16[1024,384]{1,0:T(8,128)(2,1)} %copy-done.36) | copy-start | bytes 2359300
  374.8 9.3 %copy-start.58 = (bf16[1536,1152]{1,0:T(8,128)(2,1)S(1)}, bf16[1536,1152]{1,0:T(8,128)(2,1)}, u32[]{:S(2)}) copy-start(bf16[1536,1152]{1,0:T(8,128)(2,1)} %all-gather.5.cloned.1.call-done) | copy-start | bytes 10616836
  382.6 70.6 %collective-permute-start.2 = (bf16[1024,384]{0,1:T(8,128)(2,1)}, bf16[1024,384]{0,1:T(8,128)(2,1)}, u32[]{:S(2)}, u32[]{:S(2)}) collective-permute-start(bf16[1024,384]{0,1:T(8,128)(2,1)} %constant_dynamic-slice_fusion.3), channel_id=1, source_target_pairs={{0,1},{1,0},{2,3},{3,2},{4,5},{5,4},{6,7},{7,6},{8,9},{9,8},{10,11... | collective-permute-start | bytes 2359304 | tf_op jit(solution)/shard_map/ppermute | solution.py:189
  390.6 62.6 %copy-start.21 = (bf16[1024,768]{0,1:T(8,128)(2,1)S(1)}, bf16[1024,768]{0,1:T(8,128)(2,1)}, u32[]{:S(2)}) copy-start(bf16[1024,768]{0,1:T(8,128)(2,1)} %copy-done.20) | copy-start | bytes 4718596
  391.6 64.9 %collective-permute-start.4 = (bf16[1024,384]{0,1:T(8,128)(2,1)}, bf16[1024,384]{0,1:T(8,128)(2,1)}, u32[]{:S(2)}, u32[]{:S(2)}) collective-permute-start(bf16[1024,384]{0,1:T(8,128)(2,1)} %constant_dynamic-slice_fusion), channel_id=1, source_target_pairs={{0,1},{1,0},{2,3},{3,2},{4,5},{5,4},{6,7},{7,6},{8,9},{9,8},{10,11... | collective-permute-start | bytes 2359304 | tf_op jit(solution)/shard_map/ppermute | solution.py:189
  (54 other events, 217.7 us)
Sparse Core Ops, SparseCore 0:
  11.5 66.8 all-gather.4
  81.3 52.6 all-gather.6
  136.8 62.4 all-gather.8
  202.1 61.8 all-gather.10
  298.8 95.3 reduce-scatter.6
  399.5 102.5 reduce-scatter.4
  507.6 106.6 reduce-scatter.10
  619.7 106.5 reduce-scatter.8

commit v2 on v1

--- a/solution.py
+++ b/solution.py
@@ -1,3 +1,5 @@
+from functools import partial
+
 import jax
 import jax.numpy as jnp
 from jax import lax
@@ -43,8 +45,9 @@
     return lane < HEAD
 
 
-def attend_forward_kernel(span_ref, q_ref, k_ref, v_ref, o_ref, p_ref, inv_ref, bias_ref):
-    half = q_ref.shape[0] // 2
+def attend_forward_kernel(span_ref, qkv_ref, o_ref, p_ref, inv_ref, bias_ref):
+    half = qkv_ref.shape[0] // 2
+    q_ref, k_ref, v_ref = (qkv_ref.at[:, i * PAIR : (i + 1) * PAIR] for i in range(3))
 
     @pl.when(pl.program_id(0) == 0)
     def _():
@@ -83,16 +86,6 @@
         inv_ref[part * half : (part + 1) * half, :] = jnp.where(low, invs[0], invs[1])
 
 
-def qkv_specs(length, half_blocks):
-    def spec(which):
-        return pl.BlockSpec(
-            (length, PAIR),
-            lambda j: (0, (j // half_blocks) * 3 * half_blocks + which * half_blocks + j % half_blocks),
-        )
-
-    return [spec(0), spec(1), spec(2)]
-
-
 def attend_forward(packed, spans):
     length = packed.shape[0]
     width = packed.shape[1] // 3
@@ -101,7 +94,10 @@
     return pl.pallas_call(
         attend_forward_kernel,
         grid=(pairs,),
-        in_specs=[pl.BlockSpec(memory_space=pltpu.SMEM)] + qkv_specs(length, pairs // 2),
+        in_specs=[
+            pl.BlockSpec(memory_space=pltpu.SMEM),
+            pl.BlockSpec((length, 3 * PAIR), lambda j: (0, j)),
+        ],
         out_specs=[
             pl.BlockSpec((length, PAIR), lambda j: (0, j)),
             pl.BlockSpec((1, 2, 3, half, half), lambda j: (j, 0, 0, 0, 0)),
@@ -118,17 +114,24 @@
             flops=4 * 3 * half * half * width * 4, bytes_accessed=24 << 20, transcendentals=3 * half * half * 12
         ),
         name="attend_forward",
-    )(spans, packed, packed, packed)
-
-
-def attend_backward_kernel(q_ref, k_ref, v_ref, o_ref, p_ref, inv_ref, g_ref, dq_ref, dk_ref, dv_ref):
-    half = q_ref.shape[0] // 2
+    )(spans, packed)
+
+
+def attend_backward_kernel(qkv_ref, o_ref, p_ref, inv_ref, g_ref, d_ref, sum_ref):
+    half = qkv_ref.shape[0] // 2
     low = lane_masks(half)
+    q_ref, k_ref, v_ref = (qkv_ref.at[:, i * PAIR : (i + 1) * PAIR] for i in range(3))
     dks = [None, None]
     dvs = [None, None]
+    sums = [None, None, None]
 
     def add(total, part, value):
         total[part] = value if total[part] is None else total[part] + value
+
+    def put(which, rows, value):
+        value = value.astype(bf16)
+        d_ref[rows, which * PAIR : (which + 1) * PAIR] = value
+        add(sums, which, jnp.sum(value.astype(f32), axis=0, keepdims=True))
 
     for part in range(2):
         rows = slice(part * half, (part + 1) * half)
@@ -154,11 +157,13 @@
                 dq = term if dq is None else dq + term
                 add(dks, kpart, tn(ds, qh))
                 add(dvs, kpart, tn(p, gh))
-        dq_ref[rows, :] = (dq * 0.125).astype(bf16)
+        put(0, rows, dq * 0.125)
     for part in range(2):
         rows = slice(part * half, (part + 1) * half)
-        dk_ref[rows, :] = (dks[part] * 0.125).astype(bf16)
-        dv_ref[rows, :] = dvs[part].astype(bf16)
+        put(1, rows, dks[part] * 0.125)
+        put(2, rows, dvs[part])
+    for which in range(3):
+        sum_ref[0, :, which * PAIR : (which + 1) * PAIR] = sums[which]
 
 
 def attend_backward(packed, attended, p, inv, grad_attended):
@@ -167,19 +172,22 @@
     pairs = width // PAIR
     half = length // 2
     one = pl.BlockSpec((length, PAIR), lambda j: (0, j))
+    three = pl.BlockSpec((length, 3 * PAIR), lambda j: (0, j))
     return pl.pallas_call(
         attend_backward_kernel,
         grid=(pairs,),
-        in_specs=qkv_specs(length, pairs // 2)
-        + [one, pl.BlockSpec((1, 2, 3, half, half), lambda j: (j, 0, 0, 0, 0)), one, one],
-        out_specs=[one, one, one],
-        out_shape=[jax.ShapeDtypeStruct((length, width), bf16)] * 3,
-        compiler_params=pltpu.CompilerParams(vmem_limit_bytes=60 << 20),
+        in_specs=[three, one, pl.BlockSpec((1, 2, 3, half, half), lambda j: (j, 0, 0, 0, 0)), one, one],
+        out_specs=[three, pl.BlockSpec((1, 1, 3 * PAIR), lambda j: (j, 0, 0))],
+        out_shape=[
+            jax.ShapeDtypeStruct(packed.shape, bf16),
+            jax.ShapeDtypeStruct((pairs, 1, 3 * PAIR), f32),
+        ],
+        compiler_params=pltpu.CompilerParams(vmem_limit_bytes=56 << 20),
         cost_estimate=pl.CostEstimate(
             flops=8 * 3 * half * half * width * 4, bytes_accessed=32 << 20, transcendentals=0
         ),
         name="attend_backward",
-    )(packed, packed, packed, attended, p, inv, grad_attended)
+    )(packed, attended, p, inv, grad_attended)
 
 
 SWAP = [(0, 1), (1, 0)]
@@ -212,12 +220,520 @@
     return jnp.stack([jnp.where(first, mine, other), jnp.where(first, other, mine)])
 
 
-def gather_weights(block):
-    return lax.all_gather(block, ("col", "row"), axis=0, tiled=True)
-
-
-def scatter_grad(total):
-    return lax.psum_scatter(total, ("col", "row"), scatter_dimension=0, tiled=True)
+GATHER_CUT = (0.3, 0.5)
+REDUCE_CUT = (0.34, 0.33)
+
+
+MESH = pl.DeviceIdType.MESH
+DEPTH = 4
+WAYS = ("up", "down", "y", "x", "core")
+ORDERS = ("zyx", "zxy", "xyz")
+
+
+def row_of(z, y, core):
+    return z * 4 + y * 2 + core
+
+
+def my_place():
+    row = lax.axis_index("row")
+    return row // 4, (row // 2) % 2, row % 2, lax.axis_index("col")
+
+
+def maybe(cond, act):
+    if cond is None:
+        act()
+    else:
+        pl.when(cond)(act)
+
+
+def remote(src, dst, send, recv, device):
+    return pltpu.make_async_remote_copy(
+        src_ref=src, dst_ref=dst, send_sem=send, recv_sem=recv, device_id=device, device_id_type=MESH
+    )
+
+
+def greet(always, z, up, down):
+    barrier = pltpu.get_barrier_semaphore()
+
+    def hello(device):
+        pl.semaphore_signal(barrier, inc=1, device_id=device, device_id_type=MESH)
+
+    for device in always:
+        hello(device)
+    pl.when(z < DEPTH - 1)(lambda: hello(up))
+    pl.when(z > 0)(lambda: hello(down))
+    pl.semaphore_wait(
+        barrier, len(always) + (z < DEPTH - 1).astype(jnp.int32) + (z > 0).astype(jnp.int32)
+    )
+
+
+def tree_rounds(order):
+    rounds = {}
+    for dz in (0, -1, 1, -2, 2, -3, 3):
+        for dy in (0, 1):
+            for dx in (0, 1):
+                step = {"z": dz, "y": dy, "x": dx}
+                via = None
+                for axis in order:
+                    if step[axis]:
+                        via = axis
+                onward = []
+                open_now = via is None
+                for axis in order:
+                    if axis == via:
+                        open_now = True
+                    if not open_now:
+                        continue
+                    if axis == "z":
+                        onward += ["up"] if dz <= 0 else []
+                        onward += ["down"] if dz >= 0 else []
+                    elif axis != via:
+                        onward.append(axis)
+                onward.append("core")
+                rounds.setdefault(abs(dz) + dy + dx, []).append((dz, dy, dx, onward))
+    return rounds
+
+
+def pieces_of(widths, cuts):
+    found = []
+    for part in range(3):
+        base = 0
+        for weight, width in enumerate(widths):
+            lo = max(base, cuts[part])
+            hi = min(base + width, cuts[part + 1])
+            if hi > lo:
+                found.append((part, weight, lo - cuts[part], lo - base, hi - lo))
+            base += width
+    return found
+
+
+def gather_kernel(widths, cuts, *refs):
+    count = len(widths)
+    shards = refs[:count]
+    outs = refs[count : 2 * count]
+    bufs = refs[2 * count : 2 * count + 3]
+    send, recv, local = refs[2 * count + 3 :]
+    z, y, core, x = my_place()
+    near = {
+        "up": (row_of(z + 1, y, core), x),
+        "down": (row_of(z - 1, y, core), x),
+        "y": (row_of(z, 1 - y, core), x),
+        "x": (row_of(z, y, core), 1 - x),
+        "core": (row_of(z, y, 1 - core), x),
+    }
+    has = {"up": z < DEPTH - 1, "down": z > 0}
+    pieces = pieces_of(widths, cuts)
+    row = row_of(z, y, core)
+    loads = []
+    for i, (part, weight, at, src, width) in enumerate(pieces):
+        loads.append(
+            pltpu.make_async_copy(
+                shards[weight].at[:, pl.ds(src, width)],
+                bufs[part].at[x, row, :, pl.ds(at, width)],
+                local.at[0, i],
+            )
+        )
+    for load in loads:
+        load.start()
+    greet([near["y"], near["x"], near["core"]], z, near["up"], near["down"])
+    for load in loads:
+        load.wait()
+
+    def copy(part, bz, by, bc, bx, way):
+        block = bufs[part].at[bx, row_of(bz, by, bc)]
+        slot = bx * 8 + bz * 2 + by
+        return remote(
+            block,
+            block,
+            send.at[part, slot, WAYS.index(way)],
+            recv.at[part, bx * 16 + row_of(bz, by, bc)],
+            near[way],
+        )
+
+    trees = [tree_rounds(order) for order in ORDERS]
+
+    def each(step, act):
+        for part in range(3):
+            for dz, dy, dx, onward in trees[part].get(step, []):
+                bz, by, bx = z + dz, (y + dy) % 2, (x + dx) % 2
+                cond = None if dz == 0 else ((bz >= 0) & (bz <= DEPTH - 1))
+                maybe(cond, lambda: act(part, bz, by, bx, onward))
+
+    def forward(part, bz, by, bx, onward, step):
+        if step:
+            copy(part, bz, by, core, bx, "core").wait_recv()
+        for way in onward:
+            maybe(has.get(way), lambda way=way: copy(part, bz, by, core, bx, way).start())
+
+    def finish(part, bz, by, bx, onward):
+        copy(part, bz, by, 1 - core, bx, "core").wait_recv()
+        for way in onward:
+            maybe(has.get(way), lambda way=way: copy(part, bz, by, core, bx, way).wait_send())
+
+    for step in range(6):
+        each(step, lambda *a, step=step: forward(*a, step))
+    for step in range(6):
+        each(step, finish)
+    stores = []
+    for i, (part, weight, at, src, width) in enumerate(pieces):
+        for side in range(2):
+            stores.append(
+                pltpu.make_async_copy(
+                    bufs[part].at[side, :, :, pl.ds(at, width)],
+                    outs[weight].at[:, :, pl.ds(side * widths[weight] + src, width)],
+                    local.at[1 + side, i],
+                )
+            )
+    for store in stores:
+        store.start()
+    for store in stores:
+        store.wait()
+
+
+def gather_near(shards, cuts):
+    rows = shards[0].shape[0]
+    widths = [shard.shape[1] for shard in shards]
+    outs = pl.pallas_call(
+        lambda *refs: gather_kernel(widths, cuts, *refs),
+        in_specs=[pl.BlockSpec(memory_space=pl.ANY)] * len(shards),
+        out_specs=[pl.BlockSpec(memory_space=pl.ANY)] * len(shards),
+        out_shape=[jax.ShapeDtypeStruct((16, rows, 2 * width), bf16) for width in widths],
+        scratch_shapes=[pltpu.VMEM((2, 16, rows, cuts[i + 1] - cuts[i]), bf16) for i in range(3)]
+        + [
+            pltpu.SemaphoreType.DMA((3, 16, 5)),
+            pltpu.SemaphoreType.DMA((3, 32)),
+            pltpu.SemaphoreType.DMA((3, 8)),
+        ],
+        compiler_params=pltpu.CompilerParams(
+            collective_id=0, has_side_effects=True, vmem_limit_bytes=56 << 20
+        ),
+        cost_estimate=pl.CostEstimate(flops=0, bytes_accessed=200 << 20, transcendentals=0),
+        name="gather_weights",
+    )(*shards)
+    return [out.reshape(16 * rows, 2 * width) for out, width in zip(outs, widths)]
+
+
+def reduce_kernel(widths, cuts, *refs):
+    count = len(widths)
+    grads = refs[:count]
+    small_ref = refs[count]
+    outs = refs[count + 1 : 2 * count + 1]
+    sum_ref = refs[2 * count + 1]
+    scr = refs[2 * count + 2 :]
+    acc, rcore = scr[0:3], scr[3:6]
+    rx, ry, rz, cy, cx = scr[6:8], scr[8:10], scr[10:13], scr[13], scr[14]
+    srecv, sacc, final = scr[15], scr[16], scr[17:20]
+    s_core, r_core, s_x, r_x, s_y, r_y, s_z, r_z, s_c, r_c, s_s, r_s, s_load, s_out = scr[20:]
+    z, y, core, x = my_place()
+    up, down = (row_of(z + 1, y, core), x), (row_of(z - 1, y, core), x)
+    to_y, to_x = (row_of(z, 1 - y, core), x), (row_of(z, y, core), 1 - x)
+    to_core = (row_of(z, y, 1 - core), x)
+    to_z1 = (row_of(z + 1 - 2 * (z % 2), y, core), x)
+    to_z2 = (row_of((z + 2) % 4, y, core), x)
+    pieces = pieces_of(widths, cuts)
+    by_part = [[p for p in pieces if p[0] == part] for part in range(3)]
+
+    def gcols(weight, side, src, width):
+        return pl.ds(pl.multiple_of(side * widths[weight] + src, 128), width)
+
+    loads = []
+    for i, (part, weight, at, src, width) in enumerate(pieces):
+        for side in range(2):
+            loads.append(
+                pltpu.make_async_copy(
+                    grads[weight].at[:, :, core, :, gcols(weight, side, src, width)],
+                    acc[part].at[side, :, :, :, pl.ds(at, width)],
+                    s_load.at[side, i],
+                )
+            )
+    for load in loads:
+        load.start()
+    greet([to_core, to_x, to_y, to_z2], z, up, down)
+
+    def view(part, ref, far, zi):
+        if part == 0:
+            return ref.at[(1 - x) if far else x, zi]
+        return ref.at[:, zi, (1 - y) if far else y]
+
+    def core_copies(part, far, zi):
+        copies = []
+        for i, (_, weight, at, src, width) in enumerate(by_part[part]):
+            cols = pl.ds(at, width)
+            if part == 0:
+                side = (1 - x) if far else x
+                copies.append(
+                    remote(
+                        grads[weight].at[zi, :, 1 - core, :, gcols(weight, side, src, width)],
+                        rcore[0].at[side, zi, :, :, cols],
+                        s_core.at[0, int(far), zi, i, 0],
+                        r_core.at[0, int(far), zi, i, 0],
+                        to_core,
+                    )
+                )
+            elif part == 1:
+                by = (1 - y) if far else y
+                for side in range(2):
+                    copies.append(
+                        remote(
+                            grads[weight].at[zi, by, 1 - core, :, gcols(weight, side, src, width)],
+                            rcore[1].at[side, zi, by, :, cols],
+                            s_core.at[1, int(far), zi, i, side],
+                            r_core.at[1, int(far), zi, i, side],
+                            to_core,
+                        )
+                    )
+            else:
+                for side in range(2):
+                    copies.append(
+                        remote(
+                            grads[weight].at[zi, :, 1 - core, :, gcols(weight, side, src, width)],
+                            rcore[2].at[side, zi, :, :, cols],
+                            s_core.at[2, 0, zi, i, side],
+                            r_core.at[2, 0, zi, i, side],
+                            to_core,
+                        )
+                    )
+        return copies
+
+    def loop(act):
+        def step(zi, carry):
+            act(zi)
+            return carry
+
+        lax.fori_loop(0, DEPTH, step, 0)
+
+    def start_far(zi):
+        for part in range(3):
+            for copy in core_copies(part, True, zi):
+                copy.start()
+
+    def start_near(zi):
+        for part in range(2):
+            for copy in core_copies(part, False, zi):
+                copy.start()
+
+    loop(start_far)
+    loop(start_near)
+    partners = [to_core, to_x, to_y, to_z1, to_z2]
+    sacc[0] = small_ref[...]
+
+    def small_copy(step):
+        return remote(sacc.at[step], srecv.at[step], s_s.at[step], r_s.at[step], partners[step])
+
+    def small_next(step):
+        small_copy(step).wait()
+        sacc[step + 1] = sacc[step] + srecv[step]
+        if step < 4:
+            small_copy(step + 1).start()
+
+    small_copy(0).start()
+    for load in loads:
+        load.wait()
+
+    def add(total, term):
+        total[...] = total[...] + term[...]
+
+    first = [(rx[0], s_x, r_x, to_x), (ry[0], s_y, r_y, to_y)]
+    second = [(ry[1], s_y, r_y, to_y), (rx[1], s_x, r_x, to_x)]
+
+    def first_copy(part, zi):
+        buf, send, recv, device = first[part]
+        return remote(
+            view(part, acc[part], True, zi), buf.at[zi], send.at[0, zi], recv.at[0, zi], device
+        )
+
+    def half_of(part, zi, far):
+        if part == 0:
+            return acc[0].at[x, zi, (1 - y) if far else y]
+        return acc[1].at[(1 - x) if far else x, zi, y]
+
+    def second_copy(part, zi):
+        buf, send, recv, device = second[part]
+        return remote(
+            half_of(part, zi, True), buf.at[zi], send.at[1, zi], recv.at[1, zi], device
+        )
+
+    def far_step(zi):
+        for part in range(2):
+            for copy in core_copies(part, True, zi):
+                copy.wait_recv()
+            add(view(part, acc[part], True, zi), view(part, rcore[part], True, zi))
+            first_copy(part, zi).start()
+        for copy in core_copies(2, True, zi):
+            copy.wait_recv()
+        add(acc[2].at[:, zi], rcore[2].at[:, zi])
+
+    def near_step(zi):
+        for part in range(2):
+            for copy in core_copies(part, False, zi):
+                copy.wait_recv()
+            add(view(part, acc[part], False, zi), view(part, rcore[part], False, zi))
+            first_copy(part, zi).wait_recv()
+            add(view(part, acc[part], False, zi), first[part][0].at[zi])
+            second_copy(part, zi).start()
+
+    def last_step(zi):
+        for part in range(2):
+            second_copy(part, zi).wait_recv()
+            add(half_of(part, zi, False), second[part][0].at[zi])
+
+    def block(part, zi):
+        if part == 2:
+            return acc[2].at[:, zi]
+        return acc[part].at[x, zi, y]
+
+    def line_copy(part, direction, zd):
+        return remote(
+            block(part, zd),
+            rz[part].at[direction, zd],
+            s_z.at[part, direction, zd],
+            r_z.at[part, direction, zd],
+            down if direction else up,
+        )
+
+    def line_sends(parts, step):
+        for direction in range(2):
+            at = DEPTH - 1 - step if direction else step
+            for zd in (0, 1, 2) if direction else (3, 2, 1):
+                if not ((at > zd) if direction else (at < zd)):
+                    continue
+                for part in parts:
+
+                    def act(part=part, direction=direction, zd=zd):
+                        if step > 0:
+                            line_copy(part, direction, zd).wait_recv()
+                            add(block(part, zd), rz[part].at[direction, zd])
+                        line_copy(part, direction, zd).start()
+
+                    pl.when(z == at)(act)
+
+    def line_end(parts):
+        for part in parts:
+            for direction in range(2):
+
+                def act(part=part, direction=direction):
+                    line_copy(part, direction, z).wait_recv()
+                    add(block(part, z), rz[part].at[direction, z])
+
+                pl.when((z < DEPTH - 1) if direction else (z > 0))(act)
+
+    loop(far_step)
+    small_next(0)
+    line_sends([2], 0)
+    loop(near_step)
+    small_next(1)
+    line_sends([2], 1)
+    loop(last_step)
+    small_next(2)
+    line_sends([0, 1], 0)
+    line_sends([2], 2)
+    line_end([2])
+    y_copy = remote(acc[2].at[:, z, 1 - y], cy, s_c.at[0], r_c.at[0], to_y)
+    y_copy.start()
+    line_sends([0, 1], 1)
+    small_next(3)
+    y_copy.wait_recv()
+    add(acc[2].at[:, z, y], cy)
+    x_copy = remote(acc[2].at[1 - x, z, y], cx, s_c.at[1], r_c.at[1], to_x)
+    x_copy.start()
+    line_sends([0, 1], 2)
+    x_copy.wait_recv()
+    add(acc[2].at[x, z, y], cx)
+    line_end([0, 1])
+    small_next(4)
+    sum_ref[...] = sacc[5]
+    for part in range(3):
+        final[part][...] = acc[part][x, z, y].astype(f32)
+    stores = []
+    for i, (part, weight, at, src, width) in enumerate(pieces):
+        stores.append(
+            pltpu.make_async_copy(
+                final[part].at[:, pl.ds(at, width)], outs[weight].at[:, pl.ds(src, width)], s_out.at[i]
+            )
+        )
+    for store in stores:
+        store.start()
+
+    def drain(zi):
+        for part in range(3):
+            for copy in core_copies(part, True, zi):
+                copy.wait_send()
+            if part < 2:
+                for copy in core_copies(part, False, zi):
+                    copy.wait_send()
+                first_copy(part, zi).wait_send()
+                second_copy(part, zi).wait_send()
+
+    loop(drain)
+    for part in range(3):
+        for direction in range(2):
+            for zd in range(DEPTH):
+                pl.when((z > zd) if direction else (z < zd))(
+                    lambda part=part, direction=direction, zd=zd: line_copy(part, direction, zd).wait_send()
+                )
+    y_copy.wait_send()
+    x_copy.wait_send()
+    for store in stores:
+        store.wait()
+
+
+def reduce_near(grads, small, cuts, rows):
+    widths = [grad.shape[1] // 2 for grad in grads]
+    w = [cuts[i + 1] - cuts[i] for i in range(3)]
+    dma = pltpu.SemaphoreType.DMA
+
+    def low(*shape):
+        return pltpu.VMEM(shape, bf16)
+
+    scratch = [low(2, 4, 2, rows, k) for k in w] * 2
+    scratch += [low(4, 2, rows, w[0]), low(4, rows, w[1])]
+    scratch += [low(4, 2, rows, w[1]), low(4, rows, w[0])]
+    scratch += [low(2, 4, rows, w[0]), low(2, 4, rows, w[1]), low(2, 4, 2, 2, rows, w[2])]
+    scratch += [low(2, rows, w[2]), low(rows, w[2])]
+    scratch += [pltpu.VMEM((5,) + small.shape, f32), pltpu.VMEM((6,) + small.shape, f32)]
+    scratch += [pltpu.VMEM((rows, k), f32) for k in w]
+    scratch += [dma((3, 2, 4, 4, 2)), dma((3, 2, 4, 4, 2)), dma((2, 4)), dma((2, 4)), dma((2, 4)), dma((2, 4))]
+    scratch += [dma((3, 2, 4)), dma((3, 2, 4)), dma((2,)), dma((2,)), dma((5,)), dma((5,)), dma((2, 8)), dma((8,))]
+    shaped = [grad.reshape(4, 2, 2, rows, grad.shape[1]) for grad in grads]
+    any_space = pl.BlockSpec(memory_space=pl.ANY)
+    vmem = pl.BlockSpec(memory_space=pltpu.VMEM)
+    outs = pl.pallas_call(
+        lambda *refs: reduce_kernel(widths, cuts, *refs),
+        in_specs=[any_space] * len(grads) + [vmem],
+        out_specs=[any_space] * len(grads) + [vmem],
+        out_shape=[jax.ShapeDtypeStruct((rows, width), f32) for width in widths]
+        + [jax.ShapeDtypeStruct(small.shape, f32)],
+        scratch_shapes=scratch,
+        compiler_params=pltpu.CompilerParams(
+            collective_id=1, has_side_effects=True, vmem_limit_bytes=56 << 20
+        ),
+        cost_estimate=pl.CostEstimate(flops=0, bytes_accessed=200 << 20, transcendentals=0),
+        name="reduce_grads",
+    )(*shaped, small)
+    return outs[:-1], outs[-1]
+
+
+def gather_far(shards):
+    fulls = []
+    for shard in shards:
+        rows = lax.all_gather(shard, ("col", "row"), axis=0, tiled=True)
+        fulls.append(jnp.concatenate(jnp.split(rows, 2, axis=0), axis=1))
+    return fulls
+
+
+def reduce_far(grads, small):
+    outs = []
+    for grad in grads:
+        halves = jnp.concatenate(jnp.split(grad, 2, axis=1), axis=0)
+        outs.append(lax.psum_scatter(halves, ("col", "row"), scatter_dimension=0, tiled=True).astype(f32))
+    return outs, lax.psum(small, ("row", "col"))
+
+
+def part_cuts(widths, first, second):
+    total = sum(widths) // 128
+    one = round(total * first)
+    two = round(total * (first + second))
+    return [0, one * 128, two * 128, total * 128]
 
 
 def layer_norm(value):
@@ -236,22 +752,26 @@
     return back, jnp.sum(grad * centred, axis=0), jnp.sum(grad, axis=0)
 
 
+def by_pairs(block):
+    rows, three, half = block.shape
+    return block.reshape(rows, three, half // PAIR, PAIR).transpose(0, 2, 1, 3).reshape(rows, three * half)
+
+
 def body(
-    x_in, span_start, span_kind, ln1_gain, ln1_bias, w_qkv, b_query, b_value, w_out, b_out,
+    near, x_in, span_start, span_kind, ln1_gain, ln1_bias, w_qkv, b_query, b_value, w_out, b_out,
     ln2_gain, ln2_bias, w_fc, b_fc, w_proj, b_proj, cotangent,
 ):
     half_width = x_in.shape[2]
-    width = 2 * half_width
-    ff_half = w_fc.shape[1]
     shard = w_qkv.shape[0]
     col = lax.axis_index("col")
 
-    qkv_all = gather_weights(w_qkv.reshape(shard, 3 * half_width)).reshape(2, width, 3 * half_width)
     residual = own_micro(x_in).astype(f32)
-    out_all = gather_weights(w_out.T).reshape(2, width, half_width)
-    fc_all = gather_weights(w_fc).reshape(2, width, ff_half)
-    proj_all = gather_weights(w_proj.T).reshape(2, width, ff_half)
     grad_out = own_micro(cotangent)
+    shards = [by_pairs(w_qkv), w_out.T, w_fc, w_proj.T]
+    if near:
+        qkv_all, out_all, fc_all, proj_all = gather_near(shards, part_cuts([s.shape[1] for s in shards], *GATHER_CUT))
+    else:
+        qkv_all, out_all, fc_all, proj_all = gather_far(shards)
 
     vectors = [ln1_gain, ln1_bias, b_query, b_value, b_out, ln2_gain, ln2_bias, b_fc, b_proj]
     flat = jnp.concatenate(vectors)
@@ -269,66 +789,52 @@
 
     centred_first, inverse_first = layer_norm(residual)
     normed_first = (centred_first * ln1_gain + ln1_bias).astype(bf16)
-    zero = jnp.zeros((half_width,), f32)
-    pieces = []
-    for h in range(2):
-        part = slice(h * half_width, (h + 1) * half_width)
-        bias = jnp.concatenate([b_query[part], zero, b_value[part]])
-        pieces.append((nn(normed_first, qkv_all[h]) + bias).astype(bf16))
-    packed = jnp.concatenate(pieces, axis=1)
+    bias = jnp.stack([b_query, jnp.zeros_like(b_query), b_value]).reshape(3, -1, PAIR)
+    packed = (nn(normed_first, qkv_all) + bias.transpose(1, 0, 2).reshape(-1)).astype(bf16)
     attended, p, inv = attend_forward(packed, spans)
-    branch = nt(attended[:, :half_width], out_all[0]) + nt(attended[:, half_width:], out_all[1])
-    middle = residual + branch + b_out
+    middle = residual + nt(attended, out_all) + b_out
     centred_second, inverse_second = layer_norm(middle)
     normed_second = (centred_second * ln2_gain + ln2_bias).astype(bf16)
-    branch = None
-    slopes = []
-    actives = []
-    for h in range(2):
-        hidden = nn(normed_second, fc_all[h]) + b_fc[h * ff_half : (h + 1) * ff_half]
-        squared = hidden * hidden
-        tanh = jnp.tanh(GELU_A * hidden * (1.0 + GELU_B * squared))
-        active = (0.5 * hidden * (1.0 + tanh)).astype(bf16)
-        slope = 0.5 * (1.0 + tanh) + 0.5 * hidden * (1.0 - tanh * tanh) * GELU_A * (
-            1.0 + 3.0 * GELU_B * squared
-        )
-        slopes.append(slope.astype(bf16))
-        actives.append(active)
-        term = nt(active, proj_all[h])
-        branch = term if branch is None else branch + term
-    layer_out = back_micro((middle + branch + b_proj).astype(bf16))
+    hidden = nn(normed_second, fc_all) + b_fc
+    squared = hidden * hidden
+    tanh = jnp.tanh(GELU_A * hidden * (1.0 + GELU_B * squared))
+    active = (0.5 * hidden * (1.0 + tanh)).astype(bf16)
+    slope = (
+        0.5 * (1.0 + tanh)
+        + 0.5 * hidden * (1.0 - tanh * tanh) * GELU_A * (1.0 + 3.0 * GELU_B * squared)
+    ).astype(bf16)
+    layer_out = back_micro((middle + nt(active, proj_all) + b_proj).astype(bf16))
 
     grad_out_wide = grad_out.astype(f32)
-    g_proj = [tn(grad_out, active).astype(bf16) for active in actives]
-    grad_hidden = [(nn(grad_out, proj_all[h]) * slopes[h].astype(f32)).astype(bf16) for h in range(2)]
-    g_fc = [tn(normed_second, grad) for grad in grad_hidden]
-    g_bfc = jnp.concatenate([jnp.sum(grad.astype(f32), axis=0) for grad in grad_hidden])
-    out_proj = scatter_grad(jnp.concatenate([g.astype(bf16) for g in g_proj], axis=0))
-    out_fc = scatter_grad(jnp.concatenate([g.astype(bf16) for g in g_fc], axis=0))
-    grad_normed = nt(grad_hidden[0], fc_all[0]) + nt(grad_hidden[1], fc_all[1])
+    g_proj = tn(grad_out, active).astype(bf16)
+    grad_hidden = (nn(grad_out, proj_all) * slope.astype(f32)).astype(bf16)
+    g_fc = tn(normed_second, grad_hidden).astype(bf16)
+    g_bfc = jnp.sum(grad_hidden.astype(f32), axis=0)
+    grad_normed = nt(grad_hidden, fc_all)
     back, g_ln2_gain, g_ln2_bias = norm_backward(grad_normed, centred_second, inverse_second, ln2_gain)
     grad_middle = grad_out_wide + back
     g_bproj = jnp.sum(grad_out_wide, axis=0)
     g_bout = jnp.sum(grad_middle, axis=0)
     grad_low = grad_middle.astype(bf16)
-    g_out = [tn(grad_low, attended[:, h * half_width : (h + 1) * half_width]) for h in range(2)]
-    out_out = scatter_grad(jnp.concatenate([g.astype(bf16) for g in g_out], axis=0))
-    grad_attended = jnp.concatenate([nn(grad_low, out_all[h]).astype(bf16) for h in range(2)], axis=1)
-    dq, dk, dv = attend_backward(packed, attended, p, inv, grad_attended)
-    g_bquery = jnp.sum(dq.astype(f32), axis=0)
-    g_bvalue = jnp.sum(dv.astype(f32), axis=0)
-    grad_packed = []
-    for h in range(2):
-        part = slice(h * half_width, (h + 1) * half_width)
-        grad_packed.append(jnp.concatenate([dq[:, part], dk[:, part], dv[:, part]], axis=1))
-    g_qkv = [tn(normed_first, grad) for grad in grad_packed]
-    out_qkv = scatter_grad(jnp.concatenate([g.astype(bf16) for g in g_qkv], axis=0))
-    grad_normed = nt(grad_packed[0], qkv_all[0]) + nt(grad_packed[1], qkv_all[1])
+    g_out = tn(grad_low, attended).astype(bf16)
+    grad_attended = nn(grad_low, out_all).astype(bf16)
+    grad_packed, g_bpacked = attend_backward(packed, attended, p, inv, grad_attended)
+    g_bquery = g_bpacked[:, 0, :PAIR].reshape(-1)
+    g_bvalue = g_bpacked[:, 0, 2 * PAIR :].reshape(-1)
+    g_qkv = tn(normed_first, grad_packed).astype(bf16)
+    grad_normed = nt(grad_packed, qkv_all)
     back, g_ln1_gain, g_ln1_bias = norm_backward(grad_normed, centred_first, inverse_first, ln1_gain)
     grad_input = back_micro((grad_middle + back).astype(bf16))
 
     small = [g_ln1_gain, g_ln1_bias, g_bquery, g_bvalue, g_bout, g_ln2_gain, g_ln2_bias, g_bfc, g_bproj]
-    summed = lax.psum(jnp.concatenate(small), ("row", "col"))
+    flat = jnp.concatenate(small).reshape(-1, 128)
+    grads = [g_qkv, g_out, g_fc, g_proj]
+    if near:
+        outs, summed = reduce_near(grads, flat, part_cuts([g.shape[1] // 2 for g in grads], *REDUCE_CUT), shard)
+    else:
+        outs, summed = reduce_far(grads, flat)
+    out_qkv, out_out, out_fc, out_proj = outs
+    summed = summed.reshape(-1)
     kept = []
     at = 0
     for vector in small:
@@ -340,16 +846,16 @@
         grad_input,
         kept[0],
         kept[1],
-        out_qkv.astype(f32).reshape(shard, 3, half_width),
+        out_qkv.reshape(shard, -1, 3, PAIR).transpose(0, 2, 1, 3).reshape(shard, 3, half_width),
         kept[2],
         kept[3],
-        out_out.astype(f32).T,
+        out_out.T,
         kept[4],
         kept[5],
         kept[6],
-        out_fc.astype(f32),
+        out_fc,
         kept[7],
-        out_proj.astype(f32).T,
+        out_proj.T,
         kept[8],
     )
 
@@ -360,8 +866,9 @@
         P("row", None, "col"), P("col"), P("col"), P("col", "row"), P("col"), P("col"), P("col"),
         P("row", "col"), P("col"), P("col", "row"), P("col"), P(None, "row", "col"),
     )
+    near = mesh.shape["row"] == 16
     return jax.shard_map(
-        body,
+        partial(body, near),
         mesh=mesh,
         in_specs=placed,
         out_specs=(

time: 742 us -> 393 us (0.53)
  waiting for transfers between devices: 446 us -> 0.01 us
  Pallas kernels: 48.7 us -> 239 us
  blocking collectives: 58.5 us -> 0 us
  other arithmetic: 34.1 us -> 15.4 us
  between operations: 15.8 us -> 1.91 us
    reduce_scatter x4 -> x0, waiting for transfers between devices: 262 us -> none  [scatter_grad(): lax.psum_scatter(total, ('col', 'row'), scatter_dimension=0, tiled=True)]
    pallas_call x1 -> x3, Pallas kernels: 27.2 us -> 217 us  [the longest x1 101 us: reduce_near(): pl.pallas_call(lambda *refs: reduce_kernel(widths, cuts, *refs), in_specs...]
    all_gather x4 -> x0, waiting for transfers between devices: 147 us -> none  [gather_weights(): return lax.all_gather(block, ('col', 'row'), axis=0, tiled=True)]
    psum x1 -> x0, blocking collectives: 58.5 us -> none  [body(): summed = lax.psum(jnp.concatenate(small), ('row', 'col'))]
    ppermute x5, waiting for transfers between devices: 35.9 us -> 0.01 us  [swap(): return lax.ppermute(value, 'col', SWAP)]
    concatenate x7 -> x0, other arithmetic: 12 us -> none  [the longest x1 2.48 us: body(): jnp.concatenate([g.astype(bf16) for g in g_fc], axis=0)]
    dot_general x8 -> x4, matrix products: 38.8 us -> 41.7 us  [nn(): lax.dot_general(a, b, (((1,), (0,)), ((), ())), preferred_element_type=f32)]
    dot_general x8 -> x4, matrix products: 26.9 us -> 25.9 us  [tn(): lax.dot_general(a, b, (((0,), (0,)), ((), ())), preferred_element_type=f32)]
  transfers between devices with their start and end apart: 13 -> 5, of which waited for: 9 -> 0; matrix products, arithmetic and copies ran while one was open for 16% -> 4% of each run, Pallas kernels for 7% -> 49%
where the time goes in v2:
time: 393 us; the launch traced here: 388 us
  Pallas kernels  239 us (61%)
  matrix products  98.1 us (25%)
  local copies, waits for them, and re-layouts  26.8 us (7%)
  other arithmetic  15.4 us (4%)
  starting transfers between devices  7.14 us (2%)
    pallas_call x1, Pallas kernels, reduce_near(): pl.pallas_call(lambda *refs: reduce_kernel(widths, cuts, *refs), in_specs...  101 us
    pallas_call x1, Pallas kernels, gather_near(): pl.pallas_call(lambda *refs: gather_kernel(widths, cuts, *refs), in_specs...  89.4 us
    dot_general x4, matrix products, nn(): lax.dot_general(a, b, (((1,), (0,)), ((), ())), preferred_element_type=f32)  41.7 us
    dot_general x4, matrix products, nt(): lax.dot_general(a, b, (((1,), (1,)), ((), ())), preferred_element_type=f32)  30.4 us
    pallas_call x1, Pallas kernels, attend_backward(): pl.pallas_call(attend_backward_kernel, grid=(pairs,), in_specs=[three, on...  27.4 us
    dot_general x4, matrix products, tn(): lax.dot_general(a, b, (((0,), (0,)), ((), ())), preferred_element_type=f32)  25.9 us
    pallas_call x1, Pallas kernels, attend_forward(): pl.pallas_call(attend_forward_kernel, grid=(pairs,), in_specs=[pl.BlockSp...  21.2 us
  transfers between devices with their start and end apart: 5, of which 0 were waited for; matrix products, arithmetic and copies ran while one was open for 4% of the time, Pallas kernels for 49%

profile of v2, /device:TPU:0, one launch (start us, length us, event | category | flops | bytes accessed | tf_op | source)
XLA Modules:
  0.0 387.8 jit_solution(1798093747017834891)
XLA Ops:
  3.5 3.0 collective-permute-start
  9.4 2.1 collective-permute-start.1
  13.6 89.4 %gather_weights.1 = (bf16[16,48,2304]{2,1,0:T(8,128)(2,1)}, bf16[16,48,768]{2,1,0:T(8,128)(2,1)}, bf16[16,48,3072]{2,1,0:T(8,128)(2,1)}, bf16[16,48,3072]{2,1,0:T(8,128)(2,1)}) custom-call(bf16[48,1152]{1,0:T(8,128)(2,1)} %reshape.139.refs_0_, bf16[48,384]{1,0:T(8,128)(2,1)} %bitcast.73, bf16[48,1536]{1,0:T(8,128)(2,1)} %refs_2_.1, bf16[48,1536]{1,0:T(8,128)(2,1)} %bitcast.71), custom_call_target="tpu_custom_call" | custom-call | bytes 209715200 | tf_op jit(solution)/shard_map/gather_weights/pallas_call | solution.py:396
  104.2 3.2 bitcast_select_fusion.1
  107.9 6.4 %add_convert_fusion.1.qkv_ref = bf16[1024,2304]{1,0:T(8,128)(2,1)} fusion(bf16[768,2304]{1,0:T(8,128)(2,1)S(1)} %bitcast.85, f32[2304]{0:T(1024)S(1)} %add.164, f32[768]{0:T(1024)S(1)} %get-tuple-element.159, f32[768]{0:T(1024)S(1)} %get-tuple-element.158, f32[1024]{0:T(1024)S(1)} %get-tuple-element.143, f32[1024]{0:T(1024)S(1)} %get-tuple-element.142, ...), kind=kOutput, calls=%fused_computation.5 | convolution fusion | flops 3635675136 | bytes 9853952 | tf_op jit(solution)/shard_map/dot_general | solution.py:21
  114.3 21.2 %attend_forward.1 = (bf16[1024,768]{1,0:T(8,128)(2,1)}, bf16[6,2,3,512,512]{4,3,2,1,0:T(8,128)(2,1)}, f32[1024,768]{1,0:T(8,128)}) custom-call(s32[2,2]{1,0:T(2,128)} %pad_add_fusion.span_ref, bf16[1024,2304]{1,0:T(8,128)(2,1)} %add_convert_fusion.1.qkv_ref), custom_call_target="tpu_custom_call" | custom-call | flops 9663676416 | bytes 25165824 | tf_op jit(solution)/shard_map/attend_forward/pallas_call | solution.py:94
  135.5 3.1 fusion.22
  138.7 16.2 %multiply_convert_fusion.1 = (bf16[1024,3072]{1,0:T(8,128)(2,1)}, f32[1024,3072]{1,0:T(8,128)}) fusion(f32[3072]{0:T(1024)S(1)} %pad_maximum_fusion.4, bf16[768,3072]{1,0:T(8,128)(2,1)} %bitcast.81, f32[1024,768]{0,1:T(8,128)S(1)} %get-tuple-element.87, f32[768]{0:T(1024)S(1)} %pad_maximum_fusion.11, f32[768]{0:T(1024)S(1)} %get-tuple-element.156, ...), kind=kOutput, calls=%fused_computation.3 | convolution fusion | flops 4867227648 | bytes 26765312 | tf_op jit(solution)/shard_map/dot_general | solution.py:21
  154.9 16.5 %convert_reduce_fusion = (f32[3072]{0:T(1024)S(1)}, bf16[1024,3072]{1,0:T(8,128)(2,1)}) fusion(f32[1024,3072]{1,0:T(8,128)} %get-tuple-element.145, f32[3072]{0:T(1024)S(1)} %pad_maximum_fusion.4, bf16[768,3072]{1,0:T(8,128)(2,1)S(1)} %bitcast.80, bf16[1024,384]{0,1:T(8,128)(2,1)S(1)} %copy-done.15, bf16[1024,384]{0,1:T(8,128)(2,1)S(1)} %copy-done.14), kind=kOutput, calls=%fused_computation | convolution fusion | flops 4907332608 | bytes 25190400 | tf_op jit(solution)/shard_map/dot_general | solution.py:21
  171.4 8.9 %fusion.27 = (f32[768]{0:T(1024)S(1)}, f32[1024,768]{1,0:T(8,128)}) fusion(bf16[1024,3072]{1,0:T(8,128)(2,1)} %get-tuple-element.151, bf16[768,3072]{1,0:T(8,128)(2,1)S(1)} %bitcast.84), kind=kOutput, calls=%fused_computation.126 | convolution fusion | flops 4832623616 | bytes 14158848 | tf_op jit(solution)/shard_map/dot_general | solution.py:25
  180.4 7.2 %convolution_convert_fusion.1 = bf16[768,3072]{1,0:T(8,128)(2,1)} fusion(bf16[1024,3072]{1,0:T(8,128)(2,1)S(1)} %copy-done.39, f32[1024,768]{0,1:T(8,128)S(1)} %get-tuple-element.87, f32[768]{0:T(1024)S(1)} %pad_maximum_fusion.11, f32[768]{0:T(1024)S(1)} %get-tuple-element.156, f32[1024]{0:T(1024)S(1)} %get-tuple-element.141, f32[1024]{0:T(1024)S(1)} %get-tuple-element.140), kind=kOutput, calls=%fused_computation.11 | convolution fusion | flops 4838129664 | bytes 14170112 | tf_op jit(solution)/shard_map/dot_general | solution.py:29
  187.6 3.5 copy.51
  191.1 4.0 %multiply_reduce_fusion = (f32[768]{0:T(1024)S(1)}, f32[1024]{0:T(1024)S(1)}, f32[1024]{0:T(1024)S(1)}) fusion(f32[1024,768]{0,1:T(8,128)} %copy.51, f32[1024,768]{0,1:T(8,128)} %copy-done.7, f32[1024]{0:T(1024)S(1)} %get-tuple-element.141, f32[1024]{0:T(1024)S(1)} %get-tuple-element.140, f32[768]{0:T(1024)S(1)} %get-tuple-element.156), kind=kLoop, calls=%fused_computation.30 | loop fusion | flops 6288640 | bytes 6313984 | tf_op jit(solution)/shard_map/reduce_sum | solution.py:752
  195.8 10.3 %fusion.23 = (f32[768]{0:T(1024)S(1)}, f32[1024,768]{0,1:T(8,128)S(1)}, bf16[1024,768]{0,1:T(8,128)(2,1)}, f32[768]{0:T(1024)S(1)}) fusion(f32[1024]{0:T(1024)S(1)} %broadcast_multiply_fusion.2, f32[1024,768]{0,1:T(8,128)S(1)} %copy-done.8, f32[1024]{0:T(1024)S(1)} %get-tuple-element.140, f32[1024]{0:T(1024)S(1)} %broadcast_multiply_fusion.3, ...), kind=kOutput, calls=%fused_computation.123 | convolution fusion | flops 4845205504 | bytes 23621632 | tf_op jit(solution)/shard_map/dot_general | solution.py:25
  206.1 2.6 convolution_convert_fusion.3.g_ref
  208.8 27.4 %attend_backward.1 = (bf16[1024,2304]{1,0:T(8,128)(2,1)}, f32[6,1,384]{2,1,0:T(1,128)}) custom-call(bf16[1024,2304]{1,0:T(8,128)(2,1)} %add_convert_fusion.1.qkv_ref, bf16[1024,768]{1,0:T(8,128)(2,1)} %get-tuple-element.30.o_ref, bf16[6,2,3,512,512]{4,3,2,1,0:T(8,128)(2,1)} %get-tuple-element.34.p_ref, f32[1024,768]{1,0:T(8,128)} %get-tuple-element.35.inv_ref, ...), custom_call_target="tpu_custom_call" | custom-call | flops 19327352832 | bytes 33554432 | tf_op jit(solution)/shard_map/attend_backward/pallas_call | solution.py:176
  236.2 8.0 %fusion.26 = (f32[768]{0:T(1024)S(1)}, f32[1024,768]{1,0:T(8,128)}) fusion(bf16[1024,2304]{1,0:T(8,128)(2,1)} %get-tuple-element.36, bf16[768,2304]{1,0:T(8,128)(2,1)S(1)} %bitcast.86), kind=kOutput, calls=%fused_computation.125 | convolution fusion | flops 3624664320 | bytes 11406336 | tf_op jit(solution)/shard_map/dot_general | solution.py:25
  244.2 6.3 %convolution_convert_fusion.2 = bf16[768,2304]{1,0:T(8,128)(2,1)} fusion(bf16[1024,2304]{1,0:T(8,128)(2,1)S(1)} %copy-done.40, f32[768]{0:T(1024)S(1)} %get-tuple-element.159, f32[768]{0:T(1024)S(1)} %get-tuple-element.158, f32[1024]{0:T(1024)S(1)} %get-tuple-element.143, f32[1024]{0:T(1024)S(1)} %get-tuple-element.142, ...), kind=kOutput, calls=%fused_computation.12 | convolution fusion | flops 3632726016 | bytes 9844736 | tf_op jit(solution)/shard_map/dot_general | solution.py:29
  250.5 10.0 %convolution_convert_fusion = bf16[768,3072]{1,0:T(8,128)(2,1)} fusion(bf16[1024,3072]{1,0:T(8,128)(2,1)} %get-tuple-element.144, bf16[1024,384]{0,1:T(8,128)(2,1)S(1)} %copy-done.15, bf16[1024,384]{0,1:T(8,128)(2,1)S(1)} %copy-done.14), kind=kOutput, calls=%fused_computation.10 | convolution fusion | flops 4837343232 | bytes 12582912 | tf_op jit(solution)/shard_map/dot_general | solution.py:29
  260.5 2.6 copy.52
  263.2 2.6 fusion.12
  270.3 2.4 convolution_convert_fusion.4
  273.4 100.6 %reduce_grads.1 = (f32[48,1152]{1,0:T(8,128)}, f32[48,384]{1,0:T(8,128)}, f32[48,1536]{1,0:T(8,128)}, f32[48,1536]{1,0:T(8,128)}, f32[72,128]{1,0:T(8,128)}) custom-call(bf16[4,2,2,48,2304]{4,3,2,1,0:T(8,128)(2,1)} %bitcast.65, bf16[4,2,2,48,768]{4,3,2,1,0:T(8,128)(2,1)} %bitcast.67, bf16[4,2,2,48,3072]{4,3,2,1,0:T(8,128)(2,1)} %bitcast.63, ...), custom_call_target="tpu_custom_call" | custom-call | bytes 209715200 | tf_op jit(solution)/shard_map/reduce_grads/pallas_call | solution.py:700
  380.5 1.6 copy.57
  (169 shorter events, 26.8 us)
Async XLA Ops:
  2.3 7.1 %copy-start.22 = (f32[1536]{0:T(1024)S(1)}, f32[1536]{0:T(1024)}, u32[]{:S(2)}) copy-start(f32[1536]{0:T(1024)} %param.30) | copy-start | bytes 18436
  2.3 7.1 %copy-start.28 = (f32[384]{0:T(512)S(1)}, f32[384]{0:T(512)}, u32[]{:S(2)}) copy-start(f32[384]{0:T(512)} %param.32) | copy-start | bytes 4612
  2.3 9.2 %copy-start.32 = (s32[2,1,2]{2,1,0:T(1,128)S(1)}, s32[2,1,2]{2,1,0:T(1,128)}, u32[]{:S(2)}) copy-start(s32[2,1,2]{2,1,0:T(1,128)} %param.18) | copy-start | bytes 52
  2.3 9.2 %copy-start.33 = (s32[2,1,2]{2,1,0:T(1,128)S(1)}, s32[2,1,2]{2,1,0:T(1,128)}, u32[]{:S(2)}) copy-start(s32[2,1,2]{2,1,0:T(1,128)} %param.19) | copy-start | bytes 52
  3.5 99.8 %collective-permute-start = (bf16[1024,384]{0,1:T(8,128)(2,1)}, bf16[1024,384]{0,1:T(8,128)(2,1)S(1)}, u32[]{:S(2)}, u32[]{:S(2)}) collective-permute-start(bf16[1024,384]{0,1:T(8,128)(2,1)} %bitcast.1), channel_id=1, source_target_pairs={{0,1},{1,0},{2,3},{3,2},{4,5},{5,4},{6,7},{7,6},{8,9},{9,8},{10,11... | collective-permute-start | bytes 2359304 | tf_op jit(solution)/shard_map/ppermute | solution.py:197
  9.2 95.1 %collective-permute-start.3 = (bf16[1024,384]{0,1:T(8,128)(2,1)}, bf16[1024,384]{0,1:T(8,128)(2,1)}, u32[]{:S(2)}, u32[]{:S(2)}) collective-permute-start(bf16[1024,384]{0,1:T(8,128)(2,1)} %bitcast.68), channel_id=1, source_target_pairs={{0,1},{1,0},{2,3},{3,2},{4,5},{5,4},{6,7},{7,6},{8,9},{9,8},{10,11... | collective-permute-start | bytes 2359304 | tf_op jit(solution)/shard_map/ppermute | solution.py:197
  9.4 93.7 %collective-permute-start.1 = (f32[4608]{0:T(1024)S(1)}, f32[4608]{0:T(1024)S(1)}, u32[]{:S(2)}, u32[]{:S(2)}) collective-permute-start(f32[4608]{0:T(1024)S(1)} %constant_dynamic-update-slice_fusion.8), channel_id=1, source_target_pairs={{0,1},{1,0},{2,3},{3,2},{4,5},{5,4},{6,7},{7,6},{8,9},{9,8},{10,11... | collective-permute-start | bytes 55304 | tf_op jit(solution)/shard_map/ppermute | solution.py:197
  107.4 136.8 %copy-start = (bf16[1024,384]{0,1:T(8,128)(2,1)}, bf16[1024,384]{0,1:T(8,128)(2,1)S(1)}, u32[]{:S(2)}) copy-start(bf16[1024,384]{0,1:T(8,128)(2,1)S(1)} %get-tuple-element.152) | copy-start | bytes 2359300
  107.4 136.8 %copy-start.2 = (bf16[1024,384]{0,1:T(8,128)(2,1)}, bf16[1024,384]{0,1:T(8,128)(2,1)S(1)}, u32[]{:S(2)}) copy-start(bf16[1024,384]{0,1:T(8,128)(2,1)S(1)} %get-tuple-element.153) | copy-start | bytes 2359300
  114.3 21.2 %copy-start.36 = (bf16[16,48,768]{2,1,0:T(8,128)(2,1)S(1)}, bf16[16,48,768]{2,1,0:T(8,128)(2,1)}, u32[]{:S(2)}) copy-start(bf16[16,48,768]{2,1,0:T(8,128)(2,1)} %get-tuple-element.31) | copy-start | bytes 3538948
  135.5 19.4 %slice-start = ((s8[4718592]{0:T(1024)(128)(4,1)}), s8[4194304]{0:T(1024)(128)(4,1)S(1)}, s32[]{:S(2)}) async-start(s8[4718592]{0:T(1024)(128)(4,1)} %bitcast.78), calls=%async_computation | async-start | bytes 8388608
  138.7 41.7 %copy-start.7 = (f32[1024,768]{0,1:T(8,128)}, f32[1024,768]{0,1:T(8,128)S(1)}, u32[]{:S(2)}) copy-start(f32[1024,768]{0,1:T(8,128)S(1)} %get-tuple-element.87) | copy-start | bytes 9437188
  138.7 16.2 %copy-start.14 = (bf16[1024,384]{0,1:T(8,128)(2,1)S(1)}, bf16[1024,384]{0,1:T(8,128)(2,1)}, u32[]{:S(2)}) copy-start(bf16[1024,384]{0,1:T(8,128)(2,1)} %get-tuple-element.94) | copy-start | bytes 2359300
  138.7 16.2 %copy-start.15 = (bf16[1024,384]{0,1:T(8,128)(2,1)S(1)}, bf16[1024,384]{0,1:T(8,128)(2,1)}, u32[]{:S(2)}) copy-start(bf16[1024,384]{0,1:T(8,128)(2,1)} %get-tuple-element.95) | copy-start | bytes 2359300
  138.7 16.2 %slice-start.1 = ((s8[4718592]{0:T(1024)(128)(4,1)}), s8[524288]{0:T(1024)(128)(4,1)S(1)}, s32[]{:S(2)}) async-start(s8[4718592]{0:T(1024)(128)(4,1)} %bitcast.78), calls=%async_computation.1 | async-start | bytes 1048576
  138.7 32.7 %slice-start.2 = ((s8[4718592]{0:T(1024)(128)(4,1)}), s8[4194304]{0:T(1024)(128)(4,1)S(1)}, s32[]{:S(2)}) async-start(s8[4718592]{0:T(1024)(128)(4,1)} %bitcast.82), calls=%async_computation.2 | async-start | bytes 8388608
  154.9 16.5 %slice-start.3 = ((s8[4718592]{0:T(1024)(128)(4,1)}), s8[524288]{0:T(1024)(128)(4,1)S(1)}, s32[]{:S(2)}) async-start(s8[4718592]{0:T(1024)(128)(4,1)} %bitcast.82), calls=%async_computation.3 | async-start | bytes 1048576
  171.4 9.0 %copy-start.39 = (bf16[1024,3072]{1,0:T(8,128)(2,1)S(1)}, bf16[1024,3072]{1,0:T(8,128)(2,1)}, u32[]{:S(2)}) copy-start(bf16[1024,3072]{1,0:T(8,128)(2,1)} %get-tuple-element.151) | copy-start | bytes 18874372
  195.8 10.3 %copy-start.37 = (bf16[16,48,768]{2,1,0:T(8,128)(2,1)S(1)}, bf16[16,48,768]{2,1,0:T(8,128)(2,1)}, u32[]{:S(2)}) copy-start(bf16[16,48,768]{2,1,0:T(8,128)(2,1)} %get-tuple-element.31) | copy-start | bytes 3538948
  208.8 27.4 %copy-start.35 = (bf16[16,48,2304]{2,1,0:T(8,128)(2,1)S(1)}, bf16[16,48,2304]{2,1,0:T(8,128)(2,1)}, u32[]{:S(2)}) copy-start(bf16[16,48,2304]{2,1,0:T(8,128)(2,1)} %get-tuple-element.29) | copy-start | bytes 10616836
  236.2 8.0 %copy-start.40 = (bf16[1024,2304]{1,0:T(8,128)(2,1)S(1)}, bf16[1024,2304]{1,0:T(8,128)(2,1)}, u32[]{:S(2)}) copy-start(bf16[1024,2304]{1,0:T(8,128)(2,1)} %get-tuple-element.36) | copy-start | bytes 14155780
  267.2 111.6 %collective-permute-start.4 = (bf16[1024,384]{0,1:T(8,128)(2,1)S(1)}, bf16[1024,384]{0,1:T(8,128)(2,1)}, u32[]{:S(2)}, u32[]{:S(2)}) collective-permute-start(bf16[1024,384]{0,1:T(8,128)(2,1)S(1)} %constant_dynamic-slice_fusion), channel_id=1, source_target_pairs={{0,1},{1,0},{2,3},{3,2},{4,5},{5,4},{6,7},{7,6},{8,9},{9,8},{10,11... | collective-permute-start | bytes 2359304 | tf_op jit(solution)/shard_map/ppermute | solution.py:197
  269.7 112.3 %collective-permute-start.2 = (bf16[1024,384]{0,1:T(8,128)(2,1)}, bf16[1024,384]{0,1:T(8,128)(2,1)}, u32[]{:S(2)}, u32[]{:S(2)}) collective-permute-start(bf16[1024,384]{0,1:T(8,128)(2,1)} %constant_dynamic-slice_fusion.3), channel_id=1, source_target_pairs={{0,1},{1,0},{2,3},{3,2},{4,5},{5,4},{6,7},{7,6},{8,9},{9,8},{10,11... | collective-permute-start | bytes 2359304 | tf_op jit(solution)/shard_map/ppermute | solution.py:197
  273.4 105.4 %copy-start.6 = (bf16[1024,768]{0,1:T(8,128)(2,1)S(1)}, bf16[1024,768]{0,1:T(8,128)(2,1)}, u32[]{:S(2)}) copy-start(bf16[1024,768]{0,1:T(8,128)(2,1)} %copy-done.5) | copy-start | bytes 4718596
  (26 other events, 105.7 us)

commit v3 on v2

--- a/solution.py
+++ b/solution.py
@@ -117,21 +117,17 @@
     )(spans, packed)
 
 
-def attend_backward_kernel(qkv_ref, o_ref, p_ref, inv_ref, g_ref, d_ref, sum_ref):
-    half = qkv_ref.shape[0] // 2
+def attend_back_pair(qkv_ref, o_ref, p_ref, inv_ref, g_ref, sum_ref, at):
+    length = qkv_ref.shape[0]
+    half = length // 2
     low = lane_masks(half)
-    q_ref, k_ref, v_ref = (qkv_ref.at[:, i * PAIR : (i + 1) * PAIR] for i in range(3))
+    q_ref, k_ref, v_ref = (qkv_ref.at[:, at + i * PAIR : at + (i + 1) * PAIR] for i in range(3))
     dks = [None, None]
     dvs = [None, None]
-    sums = [None, None, None]
+    dqs = []
 
     def add(total, part, value):
         total[part] = value if total[part] is None else total[part] + value
-
-    def put(which, rows, value):
-        value = value.astype(bf16)
-        d_ref[rows, which * PAIR : (which + 1) * PAIR] = value
-        add(sums, which, jnp.sum(value.astype(f32), axis=0, keepdims=True))
 
     for part in range(2):
         rows = slice(part * half, (part + 1) * half)
@@ -149,7 +145,7 @@
             rowdot = jnp.sum(jnp.where(mine, scaled, 0.0), axis=1, keepdims=True)
             for kpart in range(part + 1):
                 krows = slice(kpart * half, (kpart + 1) * half)
-                p = p_ref[0, head, part + kpart]
+                p = p_ref[head, part + kpart]
                 kh = jnp.where(mine, k_ref[krows, :], zero)
                 dp = nt(gh, v_ref[krows, :])
                 ds = (p.astype(f32) * (dp - rowdot)).astype(bf16)
@@ -157,13 +153,21 @@
                 dq = term if dq is None else dq + term
                 add(dks, kpart, tn(ds, qh))
                 add(dvs, kpart, tn(p, gh))
-        put(0, rows, dq * 0.125)
-    for part in range(2):
-        rows = slice(part * half, (part + 1) * half)
-        put(1, rows, dks[part] * 0.125)
-        put(2, rows, dvs[part])
-    for which in range(3):
-        sum_ref[0, :, which * PAIR : (which + 1) * PAIR] = sums[which]
+        dqs.append(dq)
+    for which, (ref, values, scale) in enumerate(((q_ref, dqs, 0.125), (k_ref, dks, 0.125), (v_ref, dvs, 1.0))):
+        total = None
+        for part in range(2):
+            value = (values[part] * scale).astype(bf16)
+            ref[part * half : (part + 1) * half, :] = value
+            term = jnp.sum(value.astype(f32), axis=0, keepdims=True)
+            total = term if total is None else total + term
+        if which != 1:
+            sum_ref[which // 2] = total
+
+
+def attend_backward_kernel(qkv_ref, o_ref, p_ref, inv_ref, g_ref, d_ref, sum_ref):
+    d_ref[...] = qkv_ref[...]
+    attend_back_pair(d_ref, o_ref, p_ref.at[0], inv_ref, g_ref, sum_ref.at[0], 0)
 
 
 def attend_backward(packed, attended, p, inv, grad_attended):
@@ -177,15 +181,12 @@
         attend_backward_kernel,
         grid=(pairs,),
         in_specs=[three, one, pl.BlockSpec((1, 2, 3, half, half), lambda j: (j, 0, 0, 0, 0)), one, one],
-        out_specs=[three, pl.BlockSpec((1, 1, 3 * PAIR), lambda j: (j, 0, 0))],
+        out_specs=[three, pl.BlockSpec((1, 2, 1, PAIR), lambda j: (j, 0, 0, 0))],
         out_shape=[
             jax.ShapeDtypeStruct(packed.shape, bf16),
-            jax.ShapeDtypeStruct((pairs, 1, 3 * PAIR), f32),
+            jax.ShapeDtypeStruct((pairs, 2, 1, PAIR), f32),
         ],
         compiler_params=pltpu.CompilerParams(vmem_limit_bytes=56 << 20),
-        cost_estimate=pl.CostEstimate(
-            flops=8 * 3 * half * half * width * 4, bytes_accessed=32 << 20, transcendentals=0
-        ),
         name="attend_backward",
     )(packed, attended, p, inv, grad_attended)
 
@@ -413,185 +414,180 @@
     return [out.reshape(16 * rows, 2 * width) for out, width in zip(outs, widths)]
 
 
-def reduce_kernel(widths, cuts, *refs):
-    count = len(widths)
-    grads = refs[:count]
-    small_ref = refs[count]
-    outs = refs[count + 1 : 2 * count + 1]
-    sum_ref = refs[2 * count + 1]
-    scr = refs[2 * count + 2 :]
-    acc, rcore = scr[0:3], scr[3:6]
-    rx, ry, rz, cy, cx = scr[6:8], scr[8:10], scr[10:13], scr[13], scr[14]
-    srecv, sacc, final = scr[15], scr[16], scr[17:20]
-    s_core, r_core, s_x, r_x, s_y, r_y, s_z, r_z, s_c, r_c, s_s, r_s, s_load, s_out = scr[20:]
-    z, y, core, x = my_place()
-    up, down = (row_of(z + 1, y, core), x), (row_of(z - 1, y, core), x)
-    to_y, to_x = (row_of(z, 1 - y, core), x), (row_of(z, y, core), 1 - x)
-    to_core = (row_of(z, y, 1 - core), x)
-    to_z1 = (row_of(z + 1 - 2 * (z % 2), y, core), x)
-    to_z2 = (row_of((z + 2) % 4, y, core), x)
-    pieces = pieces_of(widths, cuts)
-    by_part = [[p for p in pieces if p[0] == part] for part in range(3)]
-
-    def gcols(weight, side, src, width):
-        return pl.ds(pl.multiple_of(side * widths[weight] + src, 128), width)
-
-    loads = []
-    for i, (part, weight, at, src, width) in enumerate(pieces):
-        for side in range(2):
-            loads.append(
-                pltpu.make_async_copy(
-                    grads[weight].at[:, :, core, :, gcols(weight, side, src, width)],
-                    acc[part].at[side, :, :, :, pl.ds(at, width)],
-                    s_load.at[side, i],
-                )
-            )
-    for load in loads:
-        load.start()
-    greet([to_core, to_x, to_y, to_z2], z, up, down)
-
-    def view(part, ref, far, zi):
-        if part == 0:
-            return ref.at[(1 - x) if far else x, zi]
-        return ref.at[:, zi, (1 - y) if far else y]
-
-    def core_copies(part, far, zi):
-        copies = []
-        for i, (_, weight, at, src, width) in enumerate(by_part[part]):
-            cols = pl.ds(at, width)
-            if part == 0:
-                side = (1 - x) if far else x
-                copies.append(
-                    remote(
-                        grads[weight].at[zi, :, 1 - core, :, gcols(weight, side, src, width)],
-                        rcore[0].at[side, zi, :, :, cols],
-                        s_core.at[0, int(far), zi, i, 0],
-                        r_core.at[0, int(far), zi, i, 0],
-                        to_core,
-                    )
-                )
-            elif part == 1:
-                by = (1 - y) if far else y
-                for side in range(2):
-                    copies.append(
-                        remote(
-                            grads[weight].at[zi, by, 1 - core, :, gcols(weight, side, src, width)],
-                            rcore[1].at[side, zi, by, :, cols],
-                            s_core.at[1, int(far), zi, i, side],
-                            r_core.at[1, int(far), zi, i, side],
-                            to_core,
-                        )
-                    )
-            else:
-                for side in range(2):
-                    copies.append(
-                        remote(
-                            grads[weight].at[zi, :, 1 - core, :, gcols(weight, side, src, width)],
-                            rcore[2].at[side, zi, :, :, cols],
-                            s_core.at[2, 0, zi, i, side],
-                            r_core.at[2, 0, zi, i, side],
-                            to_core,
-                        )
-                    )
-        return copies
-
-    def loop(act):
+class Reducer:
+    def __init__(self, place, grads, widths, cuts, scratch):
+        self.z, self.y, self.core, self.x = place
+        z, y, core, x = place
+        self.grads = grads
+        self.widths = widths
+        self.acc, self.rcore = scratch[0:3], scratch[3:6]
+        rx, ry, self.rz, self.cy, self.cx = scratch[6:8], scratch[8:10], scratch[10:13], scratch[13], scratch[14]
+        self.final = scratch[15:18]
+        (
+            self.s_core, self.r_core, s_x, r_x, s_y, r_y, self.s_z, self.r_z, self.s_c, self.r_c, self.s_load,
+            self.s_out,
+        ) = scratch[18:]
+        self.up, self.down = (row_of(z + 1, y, core), x), (row_of(z - 1, y, core), x)
+        self.to_y, self.to_x = (row_of(z, 1 - y, core), x), (row_of(z, y, core), 1 - x)
+        self.to_core = (row_of(z, y, 1 - core), x)
+        self.by_part = [[p for p in pieces_of(widths, cuts) if p[0] == part] for part in range(3)]
+        self.first = [(rx[0], s_x, r_x, self.to_x), (ry[0], s_y, r_y, self.to_y)]
+        self.second = [(ry[1], s_y, r_y, self.to_y), (rx[1], s_x, r_x, self.to_x)]
+
+    SCRATCH = 30
+
+    @staticmethod
+    def scratch_shapes(widths, cuts, rows):
+        w = [cuts[i + 1] - cuts[i] for i in range(3)]
+        dma = pltpu.SemaphoreType.DMA
+
+        def low(*shape):
+            return pltpu.VMEM(shape, bf16)
+
+        scratch = [low(2, 4, 2, rows, k) for k in w] * 2
+        scratch += [low(4, 2, rows, w[0]), low(4, rows, w[1])]
+        scratch += [low(4, 2, rows, w[1]), low(4, rows, w[0])]
+        scratch += [low(2, 4, rows, w[0]), low(2, 4, rows, w[1]), low(2, 4, 2, 2, rows, w[2])]
+        scratch += [low(2, rows, w[2]), low(rows, w[2])]
+        scratch += [pltpu.VMEM((rows, k), f32) for k in w]
+        scratch += [dma((3, 2, 4, 2, 2)), dma((3, 2, 4, 2, 2)), dma((2, 4)), dma((2, 4)), dma((2, 4)), dma((2, 4))]
+        scratch += [dma((3, 2, 4)), dma((3, 2, 4)), dma((2,)), dma((2,)), dma((3, 2, 2)), dma((3, 2))]
+        return scratch
+
+    def cols(self, weight, side, src, width):
+        return pl.ds(pl.multiple_of(side * self.widths[weight] + src, 128), width)
+
+    def loop(self, act):
         def step(zi, carry):
             act(zi)
             return carry
 
         lax.fori_loop(0, DEPTH, step, 0)
 
-    def start_far(zi):
-        for part in range(3):
-            for copy in core_copies(part, True, zi):
-                copy.start()
-
-    def start_near(zi):
-        for part in range(2):
-            for copy in core_copies(part, False, zi):
-                copy.start()
-
-    loop(start_far)
-    loop(start_near)
-    partners = [to_core, to_x, to_y, to_z1, to_z2]
-    sacc[0] = small_ref[...]
-
-    def small_copy(step):
-        return remote(sacc.at[step], srecv.at[step], s_s.at[step], r_s.at[step], partners[step])
-
-    def small_next(step):
-        small_copy(step).wait()
-        sacc[step + 1] = sacc[step] + srecv[step]
-        if step < 4:
-            small_copy(step + 1).start()
-
-    small_copy(0).start()
-    for load in loads:
-        load.wait()
-
-    def add(total, term):
+    def add(self, total, term):
         total[...] = total[...] + term[...]
 
-    first = [(rx[0], s_x, r_x, to_x), (ry[0], s_y, r_y, to_y)]
-    second = [(ry[1], s_y, r_y, to_y), (rx[1], s_x, r_x, to_x)]
-
-    def first_copy(part, zi):
-        buf, send, recv, device = first[part]
+    def loads(self, part):
+        return [
+            pltpu.make_async_copy(
+                self.grads[weight].at[:, :, self.core, :, self.cols(weight, side, src, width)],
+                self.acc[part].at[side, :, :, :, pl.ds(at, width)],
+                self.s_load.at[part, side, i],
+            )
+            for i, (_, weight, at, src, width) in enumerate(self.by_part[part])
+            for side in range(2)
+        ]
+
+    def view(self, part, ref, far, zi):
+        if part == 0:
+            return ref.at[(1 - self.x) if far else self.x, zi]
+        return ref.at[:, zi, (1 - self.y) if far else self.y]
+
+    def core_copies(self, part, far, zi):
+        other = 1 - self.core
+        copies = []
+        for i, (_, weight, at, src, width) in enumerate(self.by_part[part]):
+            cols = pl.ds(at, width)
+            if part == 0:
+                sides = [(1 - self.x) if far else self.x]
+            else:
+                sides = [0, 1]
+            for k, side in enumerate(sides):
+                gcols = self.cols(weight, side, src, width)
+                if part == 1:
+                    by = (1 - self.y) if far else self.y
+                    src_ref = self.grads[weight].at[zi, by, other, :, gcols]
+                    dst_ref = self.rcore[1].at[side, zi, by, :, cols]
+                else:
+                    src_ref = self.grads[weight].at[zi, :, other, :, gcols]
+                    dst_ref = self.rcore[part].at[side, zi, :, :, cols]
+                slot = (part, int(far), zi, i, k)
+                copies.append(remote(src_ref, dst_ref, self.s_core.at[slot], self.r_core.at[slot], self.to_core))
+        return copies
+
+    def start(self, parts):
+        for part in parts:
+            for load in self.loads(part):
+                load.start()
+
+        def begin(far):
+            def act(zi):
+                for part in parts:
+                    if far or part < 2:
+                        for copy in self.core_copies(part, far, zi):
+                            copy.start()
+
+            self.loop(act)
+
+        begin(True)
+        begin(False)
+
+    def first_copy(self, part, zi):
+        buf, send, recv, device = self.first[part]
+        return remote(self.view(part, self.acc[part], True, zi), buf.at[zi], send.at[0, zi], recv.at[0, zi], device)
+
+    def half_of(self, part, zi, far):
+        if part == 0:
+            return self.acc[0].at[self.x, zi, (1 - self.y) if far else self.y]
+        return self.acc[1].at[(1 - self.x) if far else self.x, zi, self.y]
+
+    def second_copy(self, part, zi):
+        buf, send, recv, device = self.second[part]
+        return remote(self.half_of(part, zi, True), buf.at[zi], send.at[1, zi], recv.at[1, zi], device)
+
+    def far(self, parts):
+        for part in parts:
+            for load in self.loads(part):
+                load.wait()
+
+        def act(zi):
+            for part in parts:
+                for copy in self.core_copies(part, True, zi):
+                    copy.wait_recv()
+                if part == 2:
+                    self.add(self.acc[2].at[:, zi], self.rcore[2].at[:, zi])
+                else:
+                    self.add(self.view(part, self.acc[part], True, zi), self.view(part, self.rcore[part], True, zi))
+                    self.first_copy(part, zi).start()
+
+        self.loop(act)
+
+    def near(self, parts):
+        def act(zi):
+            for part in parts:
+                for copy in self.core_copies(part, False, zi):
+                    copy.wait_recv()
+                mine = self.view(part, self.acc[part], False, zi)
+                self.add(mine, self.view(part, self.rcore[part], False, zi))
+                self.first_copy(part, zi).wait_recv()
+                self.add(mine, self.first[part][0].at[zi])
+                self.second_copy(part, zi).start()
+
+        self.loop(act)
+
+    def last(self, parts):
+        def act(zi):
+            for part in parts:
+                self.second_copy(part, zi).wait_recv()
+                self.add(self.half_of(part, zi, False), self.second[part][0].at[zi])
+
+        self.loop(act)
+
+    def block(self, part, zi):
+        if part == 2:
+            return self.acc[2].at[:, zi]
+        return self.acc[part].at[self.x, zi, self.y]
+
+    def line_copy(self, part, direction, zd):
         return remote(
-            view(part, acc[part], True, zi), buf.at[zi], send.at[0, zi], recv.at[0, zi], device
+            self.block(part, zd),
+            self.rz[part].at[direction, zd],
+            self.s_z.at[part, direction, zd],
+            self.r_z.at[part, direction, zd],
+            self.down if direction else self.up,
         )
 
-    def half_of(part, zi, far):
-        if part == 0:
-            return acc[0].at[x, zi, (1 - y) if far else y]
-        return acc[1].at[(1 - x) if far else x, zi, y]
-
-    def second_copy(part, zi):
-        buf, send, recv, device = second[part]
-        return remote(
-            half_of(part, zi, True), buf.at[zi], send.at[1, zi], recv.at[1, zi], device
-        )
-
-    def far_step(zi):
-        for part in range(2):
-            for copy in core_copies(part, True, zi):
-                copy.wait_recv()
-            add(view(part, acc[part], True, zi), view(part, rcore[part], True, zi))
-            first_copy(part, zi).start()
-        for copy in core_copies(2, True, zi):
-            copy.wait_recv()
-        add(acc[2].at[:, zi], rcore[2].at[:, zi])
-
-    def near_step(zi):
-        for part in range(2):
-            for copy in core_copies(part, False, zi):
-                copy.wait_recv()
-            add(view(part, acc[part], False, zi), view(part, rcore[part], False, zi))
-            first_copy(part, zi).wait_recv()
-            add(view(part, acc[part], False, zi), first[part][0].at[zi])
-            second_copy(part, zi).start()
-
-    def last_step(zi):
-        for part in range(2):
-            second_copy(part, zi).wait_recv()
-            add(half_of(part, zi, False), second[part][0].at[zi])
-
-    def block(part, zi):
-        if part == 2:
-            return acc[2].at[:, zi]
-        return acc[part].at[x, zi, y]
-
-    def line_copy(part, direction, zd):
-        return remote(
-            block(part, zd),
-            rz[part].at[direction, zd],
-            s_z.at[part, direction, zd],
-            r_z.at[part, direction, zd],
-            down if direction else up,
-        )
-
-    def line_sends(parts, step):
+    def line(self, parts, step):
         for direction in range(2):
             at = DEPTH - 1 - step if direction else step
             for zd in (0, 1, 2) if direction else (3, 2, 1):
@@ -601,116 +597,316 @@
 
                     def act(part=part, direction=direction, zd=zd):
                         if step > 0:
-                            line_copy(part, direction, zd).wait_recv()
-                            add(block(part, zd), rz[part].at[direction, zd])
-                        line_copy(part, direction, zd).start()
-
-                    pl.when(z == at)(act)
-
-    def line_end(parts):
+                            self.line_copy(part, direction, zd).wait_recv()
+                            self.add(self.block(part, zd), self.rz[part].at[direction, zd])
+                        self.line_copy(part, direction, zd).start()
+
+                    pl.when(self.z == at)(act)
+
+    def line_end(self, parts):
         for part in parts:
             for direction in range(2):
 
                 def act(part=part, direction=direction):
-                    line_copy(part, direction, z).wait_recv()
-                    add(block(part, z), rz[part].at[direction, z])
-
-                pl.when((z < DEPTH - 1) if direction else (z > 0))(act)
-
-    loop(far_step)
+                    self.line_copy(part, direction, self.z).wait_recv()
+                    self.add(self.block(part, self.z), self.rz[part].at[direction, self.z])
+
+                pl.when((self.z < DEPTH - 1) if direction else (self.z > 0))(act)
+
+    def y_copy(self):
+        return remote(self.acc[2].at[:, self.z, 1 - self.y], self.cy, self.s_c.at[0], self.r_c.at[0], self.to_y)
+
+    def x_copy(self):
+        return remote(self.acc[2].at[1 - self.x, self.z, self.y], self.cx, self.s_c.at[1], self.r_c.at[1], self.to_x)
+
+    def turn(self):
+        self.y_copy().wait_recv()
+        self.add(self.acc[2].at[:, self.z, self.y], self.cy)
+        self.x_copy().start()
+
+    def turn_end(self):
+        self.x_copy().wait_recv()
+        self.add(self.acc[2].at[self.x, self.z, self.y], self.cx)
+
+    def stores(self, outs):
+        return [
+            pltpu.make_async_copy(
+                self.final[part].at[:, pl.ds(at, width)], outs[weight].at[:, pl.ds(src, width)], self.s_out.at[part, i]
+            )
+            for part in range(3)
+            for i, (_, weight, at, src, width) in enumerate(self.by_part[part])
+        ]
+
+    def finish(self, outs):
+        for part in range(3):
+            self.final[part][...] = self.acc[part][self.x, self.z, self.y].astype(f32)
+        for store in self.stores(outs):
+            store.start()
+
+    def drain(self, outs):
+        def act(zi):
+            for part in range(3):
+                for copy in self.core_copies(part, True, zi):
+                    copy.wait_send()
+                if part < 2:
+                    for copy in self.core_copies(part, False, zi):
+                        copy.wait_send()
+                    self.first_copy(part, zi).wait_send()
+                    self.second_copy(part, zi).wait_send()
+
+        self.loop(act)
+        for part in range(3):
+            for direction in range(2):
+                for zd in range(DEPTH):
+                    pl.when((self.z > zd) if direction else (self.z < zd))(
+                        lambda part=part, direction=direction, zd=zd: self.line_copy(part, direction, zd).wait_send()
+                    )
+        self.y_copy().wait_send()
+        self.x_copy().wait_send()
+        for store in self.stores(outs):
+            store.wait()
+
+
+PAIR_ORDER = (2, 5, 0, 3, 1, 4)
+
+
+def back_kernel(shape, *refs):
+    (
+        g_out, g_fc, g_proj, packed, attended, p_all, inv_all, gatt, normed_t, w_qkv, x_all, middle, gain_ref, small_in,
+        o_qkv, o_out, o_fc, o_proj, o_sum, o_input,
+    ) = refs[:20]
+    scr = refs[20:]
+    first = Reducer.SCRATCH
+    place = my_place()
+    z, y, core, x = place
+    early = Reducer(place, [g_out, g_fc, g_proj], shape["early"], shape["early_cuts"], scr[:first])
+    qkv, o_buf, p_buf, inv_buf, g_buf, nt_buf, w_buf, x_buf, m_buf, gqkv, gi, col_sum, srecv, sacc = scr[2 * first : 2 * first + 14]
+    s_all, s_pair, s_mid, s_gi, r_gi, l_gi, s_s, r_s = scr[2 * first + 14 :]
+    late = Reducer(place, [gqkv], shape["late"], shape["late_cuts"], scr[first : 2 * first])
+    whole = [
+        pltpu.make_async_copy(packed, qkv, s_all.at[0]),
+        pltpu.make_async_copy(normed_t, nt_buf, s_all.at[1]),
+        pltpu.make_async_copy(w_qkv, w_buf, s_all.at[2]),
+        pltpu.make_async_copy(x_all, x_buf, s_all.at[3]),
+    ]
+
+    def pair_loads(step):
+        j = PAIR_ORDER[step]
+        slot = step % 2
+        cols = pl.ds(j * PAIR, PAIR)
+        return [
+            pltpu.make_async_copy(p_all.at[j], p_buf.at[slot], s_pair.at[slot, 0]),
+            pltpu.make_async_copy(attended.at[:, cols], o_buf.at[slot], s_pair.at[slot, 1]),
+            pltpu.make_async_copy(inv_all.at[:, cols], inv_buf.at[slot], s_pair.at[slot, 2]),
+            pltpu.make_async_copy(gatt.at[:, cols], g_buf.at[slot], s_pair.at[slot, 3]),
+        ]
+
+    def begin(copies):
+        for copy in copies:
+            copy.start()
+
+    def end(copies):
+        for copy in copies:
+            copy.wait()
+
+    begin(whole[:1])
+    begin(pair_loads(0))
+    begin(whole[1:])
+    to_z1 = (row_of(z + 1 - 2 * (z % 2), y, core), x)
+    to_z2 = (row_of((z + 2) % 4, y, core), x)
+    greet([early.to_core, early.to_x, early.to_y, to_z2], z, early.up, early.down)
+    early.start((0, 1, 2))
+    end(whole[:1])
+
+    def pair(step):
+        j = PAIR_ORDER[step]
+        slot = step % 2
+        if step < 5:
+            begin(pair_loads(step + 1))
+        end(pair_loads(step))
+        attend_back_pair(qkv, o_buf.at[slot], p_buf.at[slot], inv_buf.at[slot], g_buf.at[slot], col_sum.at[j], 3 * PAIR * j)
+        if step == 0:
+            end(whole[1:2])
+        cols = slice(3 * PAIR * j, 3 * PAIR * (j + 1))
+        grad = nn(nt_buf[...], qkv[:, cols]).astype(bf16)
+        gqkv[:, :, :, :, cols] = grad.reshape(gqkv.shape[:4] + (3 * PAIR,))
+
+    rows = m_buf.shape[1]
+    blocks = x_buf.shape[0] // rows
+
+    def mid_load(i):
+        return pltpu.make_async_copy(middle.at[pl.ds(i * rows, rows)], m_buf.at[i % 2], s_mid.at[i % 2])
+
+    def input_copies(i):
+        span = pl.ds(i * rows, rows)
+        return (
+            pltpu.make_async_copy(gi.at[0, span], o_input.at[x, span], l_gi.at[i]),
+            remote(gi.at[1, span], o_input.at[x, span], s_gi.at[i], r_gi.at[i], early.to_x),
+        )
+
+    sums = [None, None]
+
+    def input_block(i):
+        span = slice(i * rows, (i + 1) * rows)
+        grad = nt(qkv[span, :], w_buf[...])
+        if i + 1 < blocks:
+            mid_load(i + 1).start()
+        mid_load(i).wait()
+        value = x_buf[span, :].astype(f32)
+        width = value.shape[1]
+        average = jnp.sum(value, axis=1, keepdims=True) / width
+        square = jnp.sum(value * value, axis=1, keepdims=True) / width
+        inverse = lax.rsqrt(square - average * average + epsilon)
+        centred = (value - average) * inverse
+        scaled = grad * gain_ref[...]
+        one = jnp.sum(scaled, axis=1, keepdims=True) / width
+        two = jnp.sum(scaled * centred, axis=1, keepdims=True) / width
+        out = m_buf[i % 2] + inverse * (scaled - one - centred * two)
+        for k, term in enumerate((grad * centred, grad)):
+            term = jnp.sum(term, axis=0, keepdims=True)
+            sums[k] = term if sums[k] is None else sums[k] + term
+        half = width // 2
+        is_low = x == 0
+        gi[0, span, :] = jnp.where(is_low, out[:, :half], out[:, half:]).astype(bf16)
+        gi[1, span, :] = jnp.where(is_low, out[:, half:], out[:, :half]).astype(bf16)
+        for copy in input_copies(i):
+            copy.start()
+
+    partners = [early.to_core, early.to_x, early.to_y, to_z1, to_z2]
+
+    def small_copy(step):
+        return remote(sacc.at[step], srecv.at[step], s_s.at[step], r_s.at[step], partners[step])
+
+    def small_start():
+        sacc[0] = small_in[...]
+        at = 0
+        for k in range(2):
+            for i in range(6):
+                sacc[0, at : at + 1, :] = sums[k][:, i * PAIR : (i + 1) * PAIR]
+                at += 1
+        for k in range(2):
+            for i in range(6):
+                sacc[0, at : at + 1, :] = col_sum[i, k]
+                at += 1
+        small_copy(0).start()
+
+    def small_next(step):
+        small_copy(step).wait()
+        sacc[step + 1] = sacc[step] + srecv[step]
+        if step < 4:
+            small_copy(step + 1).start()
+
+    both = (0, 1)
+    pair(0)
+    early.far((0, 1, 2))
+    early.line((2,), 0)
+    pair(1)
+    late.start((2,))
+    early.line((2,), 1)
+    pair(2)
+    early.line((2,), 2)
+    late.far((2,))
+    late.line((2,), 0)
+    pair(3)
+    late.start((0,))
+    early.near(both)
+    early.line_end((2,))
+    early.y_copy().start()
+    late.line((2,), 1)
+    pair(4)
+    late.far((0,))
+    early.turn()
+    late.line((2,), 2)
+    mid_load(0).start()
+    pair(5)
+    late.start((1,))
+    early.last(both)
+    early.line(both, 0)
+    late.line_end((2,))
+    late.y_copy().start()
+    early.turn_end()
+    end(whole[2:])
+    input_block(0)
+    late.far((1,))
+    early.line(both, 1)
+    late.turn()
+    late.near((0,))
+    input_block(1)
+    early.line(both, 2)
+    late.turn_end()
+    late.near((1,))
+    input_block(2)
+    late.last((0,))
+    late.line((0,), 0)
+    input_block(3)
+    small_start()
+    early.line_end(both)
+    early.finish([o_out, o_fc, o_proj])
+    late.last((1,))
+    late.line((1,), 0)
     small_next(0)
-    line_sends([2], 0)
-    loop(near_step)
+    late.line(both, 1)
     small_next(1)
-    line_sends([2], 1)
-    loop(last_step)
+    late.line(both, 2)
     small_next(2)
-    line_sends([0, 1], 0)
-    line_sends([2], 2)
-    line_end([2])
-    y_copy = remote(acc[2].at[:, z, 1 - y], cy, s_c.at[0], r_c.at[0], to_y)
-    y_copy.start()
-    line_sends([0, 1], 1)
+    late.line_end(both)
+    late.finish([o_qkv])
     small_next(3)
-    y_copy.wait_recv()
-    add(acc[2].at[:, z, y], cy)
-    x_copy = remote(acc[2].at[1 - x, z, y], cx, s_c.at[1], r_c.at[1], to_x)
-    x_copy.start()
-    line_sends([0, 1], 2)
-    x_copy.wait_recv()
-    add(acc[2].at[x, z, y], cx)
-    line_end([0, 1])
     small_next(4)
-    sum_ref[...] = sacc[5]
-    for part in range(3):
-        final[part][...] = acc[part][x, z, y].astype(f32)
-    stores = []
-    for i, (part, weight, at, src, width) in enumerate(pieces):
-        stores.append(
-            pltpu.make_async_copy(
-                final[part].at[:, pl.ds(at, width)], outs[weight].at[:, pl.ds(src, width)], s_out.at[i]
-            )
-        )
-    for store in stores:
-        store.start()
-
-    def drain(zi):
-        for part in range(3):
-            for copy in core_copies(part, True, zi):
-                copy.wait_send()
-            if part < 2:
-                for copy in core_copies(part, False, zi):
-                    copy.wait_send()
-                first_copy(part, zi).wait_send()
-                second_copy(part, zi).wait_send()
-
-    loop(drain)
-    for part in range(3):
-        for direction in range(2):
-            for zd in range(DEPTH):
-                pl.when((z > zd) if direction else (z < zd))(
-                    lambda part=part, direction=direction, zd=zd: line_copy(part, direction, zd).wait_send()
-                )
-    y_copy.wait_send()
-    x_copy.wait_send()
-    for store in stores:
-        store.wait()
-
-
-def reduce_near(grads, small, cuts, rows):
-    widths = [grad.shape[1] // 2 for grad in grads]
-    w = [cuts[i + 1] - cuts[i] for i in range(3)]
+    o_sum[...] = sacc[5]
+    for i in range(blocks):
+        local, other = input_copies(i)
+        local.wait()
+        other.wait()
+    early.drain([o_out, o_fc, o_proj])
+    late.drain([o_qkv])
+
+
+def back_near(grads, packed, attended, p, inv, gatt, normed_t, w_qkv, x, middle, gain, small, rows):
+    length, width = x.shape
+    wide = packed.shape[1]
+    early = [grad.shape[1] // 2 for grad in grads]
+    shape = {"early": early, "early_cuts": part_cuts(early, *REDUCE_CUT), "late": [wide // 2]}
+    shape["late_cuts"] = [0, wide // 6, wide // 3, wide // 2]
     dma = pltpu.SemaphoreType.DMA
-
-    def low(*shape):
-        return pltpu.VMEM(shape, bf16)
-
-    scratch = [low(2, 4, 2, rows, k) for k in w] * 2
-    scratch += [low(4, 2, rows, w[0]), low(4, rows, w[1])]
-    scratch += [low(4, 2, rows, w[1]), low(4, rows, w[0])]
-    scratch += [low(2, 4, rows, w[0]), low(2, 4, rows, w[1]), low(2, 4, 2, 2, rows, w[2])]
-    scratch += [low(2, rows, w[2]), low(rows, w[2])]
-    scratch += [pltpu.VMEM((5,) + small.shape, f32), pltpu.VMEM((6,) + small.shape, f32)]
-    scratch += [pltpu.VMEM((rows, k), f32) for k in w]
-    scratch += [dma((3, 2, 4, 4, 2)), dma((3, 2, 4, 4, 2)), dma((2, 4)), dma((2, 4)), dma((2, 4)), dma((2, 4))]
-    scratch += [dma((3, 2, 4)), dma((3, 2, 4)), dma((2,)), dma((2,)), dma((5,)), dma((5,)), dma((2, 8)), dma((8,))]
+    half = length // 2
+    blocks = 4
+    scratch = Reducer.scratch_shapes(early, shape["early_cuts"], rows)
+    scratch += Reducer.scratch_shapes(shape["late"], shape["late_cuts"], rows)
+    scratch += [
+        pltpu.VMEM((length, wide), bf16),
+        pltpu.VMEM((2, length, PAIR), bf16),
+        pltpu.VMEM((2, 2, 3, half, half), bf16),
+        pltpu.VMEM((2, length, PAIR), f32),
+        pltpu.VMEM((2, length, PAIR), bf16),
+        pltpu.VMEM((width, length), bf16),
+        pltpu.VMEM((width, wide), bf16),
+        pltpu.VMEM((length, width), bf16),
+        pltpu.VMEM((2, length // blocks, width), f32),
+        pltpu.VMEM((4, 2, 2, rows, wide), bf16),
+        pltpu.VMEM((2, length, width // 2), bf16),
+        pltpu.VMEM((width // PAIR, 2, 1, PAIR), f32),
+        pltpu.VMEM((5,) + small.shape, f32),
+        pltpu.VMEM((6,) + small.shape, f32),
+    ]
+    scratch += [dma((4,)), dma((2, 4)), dma((2,)), dma((4,)), dma((4,)), dma((4,)), dma((5,)), dma((5,))]
     shaped = [grad.reshape(4, 2, 2, rows, grad.shape[1]) for grad in grads]
     any_space = pl.BlockSpec(memory_space=pl.ANY)
     vmem = pl.BlockSpec(memory_space=pltpu.VMEM)
     outs = pl.pallas_call(
-        lambda *refs: reduce_kernel(widths, cuts, *refs),
-        in_specs=[any_space] * len(grads) + [vmem],
-        out_specs=[any_space] * len(grads) + [vmem],
-        out_shape=[jax.ShapeDtypeStruct((rows, width), f32) for width in widths]
-        + [jax.ShapeDtypeStruct(small.shape, f32)],
+        lambda *refs: back_kernel(shape, *refs),
+        in_specs=[any_space] * 12 + [vmem, vmem],
+        out_specs=[any_space] * 4 + [vmem, any_space],
+        out_shape=[jax.ShapeDtypeStruct((rows, w), f32) for w in [wide // 2] + early]
+        + [jax.ShapeDtypeStruct(small.shape, f32), jax.ShapeDtypeStruct((2, length, width // 2), bf16)],
         scratch_shapes=scratch,
         compiler_params=pltpu.CompilerParams(
-            collective_id=1, has_side_effects=True, vmem_limit_bytes=56 << 20
+            collective_id=1, has_side_effects=True, vmem_limit_bytes=67043328
         ),
-        cost_estimate=pl.CostEstimate(flops=0, bytes_accessed=200 << 20, transcendentals=0),
+        cost_estimate=pl.CostEstimate(flops=30 << 30, bytes_accessed=200 << 20, transcendentals=0),
         name="reduce_grads",
-    )(*shaped, small)
-    return outs[:-1], outs[-1]
+    )(*shaped, packed, attended, p, inv, gatt, normed_t, w_qkv, x, middle, gain.reshape(1, -1), small)
+    return outs
 
 
 def gather_far(shards):
@@ -765,7 +961,9 @@
     shard = w_qkv.shape[0]
     col = lax.axis_index("col")
 
-    residual = own_micro(x_in).astype(f32)
+    x_own = own_micro(x_in)
+    width = x_own.shape[1]
+    residual = x_own.astype(f32)
     grad_out = own_micro(cotangent)
     shards = [by_pairs(w_qkv), w_out.T, w_fc, w_proj.T]
     if near:
@@ -818,21 +1016,22 @@
     grad_low = grad_middle.astype(bf16)
     g_out = tn(grad_low, attended).astype(bf16)
     grad_attended = nn(grad_low, out_all).astype(bf16)
-    grad_packed, g_bpacked = attend_backward(packed, attended, p, inv, grad_attended)
-    g_bquery = g_bpacked[:, 0, :PAIR].reshape(-1)
-    g_bvalue = g_bpacked[:, 0, 2 * PAIR :].reshape(-1)
-    g_qkv = tn(normed_first, grad_packed).astype(bf16)
-    grad_normed = nt(grad_packed, qkv_all)
-    back, g_ln1_gain, g_ln1_bias = norm_backward(grad_normed, centred_first, inverse_first, ln1_gain)
-    grad_input = back_micro((grad_middle + back).astype(bf16))
-
-    small = [g_ln1_gain, g_ln1_bias, g_bquery, g_bvalue, g_bout, g_ln2_gain, g_ln2_bias, g_bfc, g_bproj]
-    flat = jnp.concatenate(small).reshape(-1, 128)
-    grads = [g_qkv, g_out, g_fc, g_proj]
+    zeros = jnp.zeros((width,), f32)
+    small = [zeros, zeros, zeros, zeros, g_bout, g_ln2_gain, g_ln2_bias, g_bfc, g_bproj]
     if near:
-        outs, summed = reduce_near(grads, flat, part_cuts([g.shape[1] // 2 for g in grads], *REDUCE_CUT), shard)
+        flat = jnp.concatenate(small).reshape(-1, 128)
+        *outs, summed, grad_input = back_near(
+            [g_out, g_fc, g_proj], packed, attended, p, inv, grad_attended, normed_first.T, qkv_all,
+            x_own, grad_middle, ln1_gain, flat, shard,
+        )
     else:
-        outs, summed = reduce_far(grads, flat)
+        grad_packed, sums = attend_backward(packed, attended, p, inv, grad_attended)
+        g_qkv = tn(normed_first, grad_packed).astype(bf16)
+        grad_normed = nt(grad_packed, qkv_all)
+        back, g_ln1_gain, g_ln1_bias = norm_backward(grad_normed, centred_first, inverse_first, ln1_gain)
+        grad_input = back_micro((grad_middle + back).astype(bf16))
+        small[:4] = [g_ln1_gain, g_ln1_bias, sums[:, 0, 0].reshape(-1), sums[:, 1, 0].reshape(-1)]
+        outs, summed = reduce_far([g_qkv, g_out, g_fc, g_proj], jnp.concatenate(small))
     out_qkv, out_out, out_fc, out_proj = outs
     summed = summed.reshape(-1)
     kept = []

time: 393 us -> 340 us (0.87)
  Pallas kernels: 239 us -> 208 us
  matrix products: 98.1 us -> 80.9 us
  other arithmetic: 15.4 us -> 8.82 us
    pallas_call x2 -> x1, Pallas kernels: 128 us -> 102 us  [back_near(): pl.pallas_call(lambda *refs: back_kernel(shape, *refs), in_specs=[any_spa...]
    dot_general x4 -> x3, matrix products: 30.4 us -> 23.1 us  [nt(): lax.dot_general(a, b, (((1,), (1,)), ((), ())), preferred_element_type=f32)]
    unnamed x111 -> x71, local copies, waits for them, and re-layouts: 7.84 us -> 14.7 us
    reduce_sum x2 -> x0, other arithmetic: 6.56 us -> none  [norm_backward(): return (back, jnp.sum(grad * centred, axis=0), jnp.sum(grad, axis=0))]
    dot_general x2 -> x0, local copies, waits for them, and re-layouts: 6.11 us -> none  [nt(): lax.dot_general(a, b, (((1,), (1,)), ((), ())), preferred_element_type=f32)]
    dot_general x4 -> x3, matrix products: 25.9 us -> 19.9 us  [tn(): lax.dot_general(a, b, (((0,), (0,)), ((), ())), preferred_element_type=f32)]
    dynamic_slice x6 -> x0, local copies, waits for them, and re-layouts: 5.98 us -> none  [the longest x4 3.64 us: own_micro(): mine = lax.dynamic_index_in_dim(halves, col, 0, keepdims=False)]
    pallas_call x1, Pallas kernels: 89.4 us -> 84.8 us  [gather_near(): pl.pallas_call(lambda *refs: gather_kernel(widths, cuts, *refs), in_specs...]
  transfers between devices with their start and end apart: 5 -> 4, of which waited for: 0 -> 0; matrix products, arithmetic and copies ran while one was open for 4% -> 14% of each run, Pallas kernels for 49% -> 62%
where the time goes in v3:
time: 340 us; the launch traced here: 335 us
  Pallas kernels  208 us (61%)
  matrix products  80.9 us (24%)
  local copies, waits for them, and re-layouts  29.3 us (9%)
  other arithmetic  8.82 us (3%)
  starting transfers between devices  6.61 us (2%)
    pallas_call x1, Pallas kernels, back_near(): pl.pallas_call(lambda *refs: back_kernel(shape, *refs), in_specs=[any_spa...  102 us
    pallas_call x1, Pallas kernels, gather_near(): pl.pallas_call(lambda *refs: gather_kernel(widths, cuts, *refs), in_specs...  84.8 us
    dot_general x4, matrix products, nn(): lax.dot_general(a, b, (((1,), (0,)), ((), ())), preferred_element_type=f32)  37.8 us
    dot_general x3, matrix products, nt(): lax.dot_general(a, b, (((1,), (1,)), ((), ())), preferred_element_type=f32)  23.1 us
    pallas_call x1, Pallas kernels, attend_forward(): pl.pallas_call(attend_forward_kernel, grid=(pairs,), in_specs=[pl.BlockSp...  21.1 us
    dot_general x3, matrix products, tn(): lax.dot_general(a, b, (((0,), (0,)), ((), ())), preferred_element_type=f32)  19.9 us
    unnamed x71, local copies, waits for them, and re-layouts  14.7 us
  transfers between devices with their start and end apart: 4, of which 0 were waited for; matrix products, arithmetic and copies ran while one was open for 14% of the time, Pallas kernels for 62%

profile of v3, /device:TPU:0, one launch (start us, length us, event | category | flops | bytes accessed | tf_op | source)
XLA Modules:
  0.0 335.2 jit_solution(17618864641829314065)
XLA Ops:
  0.8 1.4 dynamic-slice_bitcast_fusion.1
  2.2 3.0 collective-permute-start
  12.6 2.1 collective-permute-start.3
  16.9 84.8 %gather_weights.1 = (bf16[16,48,2304]{2,1,0:T(8,128)(2,1)}, bf16[16,48,768]{2,1,0:T(8,128)(2,1)}, bf16[16,48,3072]{2,1,0:T(8,128)(2,1)}, bf16[16,48,3072]{2,1,0:T(8,128)(2,1)}) custom-call(bf16[48,1152]{1,0:T(8,128)(2,1)} %reshape.129.refs_0_, bf16[48,384]{1,0:T(8,128)(2,1)} %bitcast.60, bf16[48,1536]{1,0:T(8,128)(2,1)} %refs_2_.1, bf16[48,1536]{1,0:T(8,128)(2,1)} %bitcast.58), custom_call_target="tpu_custom_call" | custom-call | bytes 209715200 | tf_op jit(solution)/shard_map/gather_weights/pallas_call | solution.py:397
  102.6 1.6 bitcast_select_fusion.3
  104.8 6.5 %add_convert_fusion.1.qkv_ref.refs_3_ = bf16[1024,2304]{1,0:T(8,128)(2,1)} fusion(bf16[768,2304]{1,0:T(8,128)(2,1)S(1)} %bitcast.72, f32[2304]{0:T(1024)S(1)} %add.159, f32[768]{0:T(1024)S(1)} %get-tuple-element.115, f32[768]{0:T(1024)S(1)} %get-tuple-element.114, f32[1024]{0:T(1024)S(1)} %get-tuple-element.102, f32[1024]{0:T(1024)S(1)} %get-tuple-element.101, ...), kind=kOutput, calls=%fused_computation.5 | convolution fusion | flops 3635675136 | bytes 9853952 | tf_op jit(solution)/shard_map/dot_general | solution.py:21
  111.3 21.1 %attend_forward.1 = (bf16[1024,768]{1,0:T(8,128)(2,1)}, bf16[6,2,3,512,512]{4,3,2,1,0:T(8,128)(2,1)}, f32[1024,768]{1,0:T(8,128)}) custom-call(s32[2,2]{1,0:T(2,128)} %pad_add_fusion.span_ref, bf16[1024,2304]{1,0:T(8,128)(2,1)} %add_convert_fusion.1.qkv_ref.refs_3_), custom_call_target="tpu_custom_call" | custom-call | flops 9663676416 | bytes 25165824 | tf_op jit(solution)/shard_map/attend_forward/pallas_call | solution.py:94
  132.4 4.4 %fusion.13 = (f32[1024]{0:T(1024)S(1)}, f32[1024]{0:T(1024)S(1)}, f32[1024,768]{1,0:T(8,128)S(1)}, bf16[768,1024]{0,1:T(8,128)(2,1)S(1)}) fusion(f32[768]{0:T(1024)S(1)} %pad_maximum_fusion.8, bf16[1024,384]{1,0:T(8,128)(2,1)S(1)} %get-tuple-element.58, bf16[1024,384]{1,0:T(8,128)(2,1)S(1)} %get-tuple-element.57, f32[768]{0:T(1024)S(1)} %get-tuple-element.115, ...), kind=kOutput, calls=%fused_computation.99 | convolution fusion | flops 1218967552 | bytes 9069568 | tf_op jit(solution)/shard_map/dot_general | solution.py:25
  136.9 13.8 %multiply_convert_fusion.1 = (bf16[1024,3072]{1,0:T(8,128)(2,1)}, f32[1024,3072]{1,0:T(8,128)}) fusion(f32[3072]{0:T(1024)S(1)} %pad_maximum_fusion.3, bf16[768,3072]{1,0:T(8,128)(2,1)} %bitcast.67, f32[1024,768]{1,0:T(8,128)S(1)} %get-tuple-element.51, f32[768]{0:T(1024)S(1)} %pad_maximum_fusion.10, f32[768]{0:T(1024)S(1)} %get-tuple-element.110, ...), kind=kOutput, calls=%fused_computation.3 | convolution fusion | flops 4867227648 | bytes 26765312 | tf_op jit(solution)/shard_map/dot_general | solution.py:21
  150.6 1.4 bitcast_select_fusion.1
  152.1 15.0 %convert_reduce_fusion = (f32[3072]{0:T(1024)S(1)}, bf16[1024,3072]{1,0:T(8,128)(2,1)}) fusion(f32[1024,3072]{1,0:T(8,128)} %get-tuple-element.105, f32[3072]{0:T(1024)S(1)} %pad_maximum_fusion.3, bf16[768,3072]{1,0:T(8,128)(2,1)S(1)} %bitcast.65, bf16[1024,384]{1,0:T(8,128)(2,1)S(1)} %get-tuple-element.54, bf16[1024,384]{1,0:T(8,128)(2,1)S(1)} %get-tuple-element.53), kind=kOutput, calls=%fused_computation | convolution fusion | flops 4907332608 | bytes 25190400 | tf_op jit(solution)/shard_map/dot_general | solution.py:21
  167.1 9.3 %multiply_reduce_fusion = (f32[768]{0:T(1024)S(1)}, f32[1024]{0:T(1024)S(1)}, f32[1024]{0:T(1024)S(1)}, f32[768]{0:T(1024)S(1)}, f32[1024,768]{1,0:T(8,128)}) fusion(f32[1024,768]{1,0:T(8,128)S(1)} %get-tuple-element.51, f32[1024]{0:T(1024)S(1)} %get-tuple-element.100, f32[1024]{0:T(1024)S(1)} %get-tuple-element.99, f32[768]{0:T(1024)S(1)} %get-tuple-element.110, ...), kind=kOutput, calls=%fused_computation.20 | convolution fusion | flops 4838912000 | bytes 17327104 | tf_op jit(solution)/shard_map/dot_general | solution.py:25
  176.4 7.7 %convolution_convert_fusion.1 = bf16[768,3072]{1,0:T(8,128)(2,1)} fusion(bf16[1024,3072]{1,0:T(8,128)(2,1)S(1)} %copy-done.21, f32[1024,768]{1,0:T(8,128)S(1)} %get-tuple-element.51, f32[768]{0:T(1024)S(1)} %pad_maximum_fusion.10, f32[768]{0:T(1024)S(1)} %get-tuple-element.110, f32[1024]{0:T(1024)S(1)} %get-tuple-element.100, f32[1024]{0:T(1024)S(1)} %get-tuple-element.99), kind=kOutput, calls=%fused_computation.11 | convolution fusion | flops 4838129664 | bytes 14170112 | tf_op jit(solution)/shard_map/dot_general | solution.py:29
  184.1 9.4 %fusion.14 = (f32[768]{0:T(1024)S(1)}, f32[1024,768]{1,0:T(8,128)S(1)}, bf16[1024,768]{1,0:T(8,128)(2,1)}, f32[768]{0:T(1024)S(1)}) fusion(f32[1024]{0:T(1024)S(1)} %broadcast_multiply_fusion, f32[1024,768]{1,0:T(8,128)S(1)} %get-tuple-element.51, f32[1024]{0:T(1024)S(1)} %get-tuple-element.99, f32[1024]{0:T(1024)S(1)} %broadcast_multiply_fusion.1, ...), kind=kOutput, calls=%fused_computation.100 | convolution fusion | flops 4845205504 | bytes 23621632 | tf_op jit(solution)/shard_map/dot_general | solution.py:25
  193.6 2.6 convolution_convert_fusion.2.refs_7_
  196.2 2.5 convolution_convert_fusion.3
  198.7 9.7 %convolution_convert_fusion = bf16[768,3072]{1,0:T(8,128)(2,1)} fusion(bf16[1024,3072]{1,0:T(8,128)(2,1)} %get-tuple-element.104, bf16[1024,384]{1,0:T(8,128)(2,1)S(1)} %get-tuple-element.54, bf16[1024,384]{1,0:T(8,128)(2,1)S(1)} %get-tuple-element.53), kind=kOutput, calls=%fused_computation.10 | convolution fusion | flops 4837343232 | bytes 12582912 | tf_op jit(solution)/shard_map/dot_general | solution.py:29
  209.8 1.6 copy.38.refs_8_
  211.4 2.1 constant_dynamic-slice_fusion
  213.5 1.5 collective-permute-start.2
  221.5 102.3 %reduce_grads.1 = (f32[48,1152]{1,0:T(8,128)}, f32[48,384]{1,0:T(8,128)}, f32[48,1536]{1,0:T(8,128)}, f32[48,1536]{1,0:T(8,128)}, f32[72,128]{1,0:T(8,128)}, /*index=5*/bf16[2,1024,384]{2,1,0:T(8,128)(2,1)}) custom-call(bf16[4,2,2,48,768]{4,3,2,1,0:T(8,128)(2,1)} %bitcast.77, bf16[4,2,2,48,3072]{4,3,2,1,0:T(8,128)(2,1)} %bitcast.75, ...), custom_call_target="tpu_custom_call" | custom-call | flops 32212254720 | bytes 209715200 | tf_op jit(solution)/shard_map/reduce_grads/pallas_call | solution.py:896
  325.7 1.4 dynamic_slice.68
  327.1 1.5 fusion.16
  328.6 1.8 select_bitcast_fusion.1
  (112 shorter events, 25.3 us)
Async XLA Ops:
  0.6 101.9 %copy-start.1 = (bf16[2,1024,384]{2,1,0:T(8,128)(2,1)S(1)}, bf16[2,1024,384]{2,1,0:T(8,128)(2,1)}, u32[]{:S(2)}) copy-start(bf16[2,1024,384]{2,1,0:T(8,128)(2,1)} %param.17) | copy-start | bytes 4718596
  0.7 101.2 %copy-start.14 = (f32[384]{0:T(512)S(1)}, f32[384]{0:T(512)}, u32[]{:S(2)}) copy-start(f32[384]{0:T(512)} %param.20) | copy-start | bytes 4612
  0.7 101.2 %copy-start.15 = (f32[384]{0:T(512)S(1)}, f32[384]{0:T(512)}, u32[]{:S(2)}) copy-start(f32[384]{0:T(512)} %param.21) | copy-start | bytes 4612
  0.7 101.0 %copy-start.9 = (f32[384]{0:T(512)S(1)}, f32[384]{0:T(512)}, u32[]{:S(2)}) copy-start(f32[384]{0:T(512)} %param.23) | copy-start | bytes 4612
  0.7 101.0 %copy-start.10 = (f32[384]{0:T(512)S(1)}, f32[384]{0:T(512)}, u32[]{:S(2)}) copy-start(f32[384]{0:T(512)} %param.24) | copy-start | bytes 4612
  0.7 101.0 %copy-start.11 = (f32[384]{0:T(512)S(1)}, f32[384]{0:T(512)}, u32[]{:S(2)}) copy-start(f32[384]{0:T(512)} %param.26) | copy-start | bytes 4612
  0.7 101.0 %copy-start.12 = (f32[384]{0:T(512)S(1)}, f32[384]{0:T(512)}, u32[]{:S(2)}) copy-start(f32[384]{0:T(512)} %param.27) | copy-start | bytes 4612
  0.7 101.0 %copy-start.13 = (f32[384]{0:T(512)S(1)}, f32[384]{0:T(512)}, u32[]{:S(2)}) copy-start(f32[384]{0:T(512)} %param.28) | copy-start | bytes 4612
  0.7 101.8 %copy-start.7 = (f32[1536]{0:T(1024)S(1)}, f32[1536]{0:T(1024)}, u32[]{:S(2)}) copy-start(f32[1536]{0:T(1024)} %param.30) | copy-start | bytes 18436
  0.8 100.9 %copy-start.8 = (f32[384]{0:T(512)S(1)}, f32[384]{0:T(512)}, u32[]{:S(2)}) copy-start(f32[384]{0:T(512)} %param.32) | copy-start | bytes 4612
  0.8 14.5 %copy-start.16 = (s32[2,1,2]{2,1,0:T(1,128)S(1)}, s32[2,1,2]{2,1,0:T(1,128)}, u32[]{:S(2)}) copy-start(s32[2,1,2]{2,1,0:T(1,128)} %param.18) | copy-start | bytes 52
  0.8 14.5 %copy-start.17 = (s32[2,1,2]{2,1,0:T(1,128)S(1)}, s32[2,1,2]{2,1,0:T(1,128)}, u32[]{:S(2)}) copy-start(s32[2,1,2]{2,1,0:T(1,128)} %param.19) | copy-start | bytes 52
  0.8 15.1 %copy-start.5 = (bf16[48,3,384]{2,0,1:T(8,128)(2,1)S(1)}, bf16[48,3,384]{2,0,1:T(8,128)(2,1)}, u32[]{:S(2)}) copy-start(bf16[48,3,384]{2,0,1:T(8,128)(2,1)} %param.22) | copy-start | bytes 331780
  2.2 100.4 %collective-permute-start = (bf16[1024,384]{1,0:T(8,128)(2,1)S(1)}, bf16[1024,384]{1,0:T(8,128)(2,1)}, u32[]{:S(2)}, u32[]{:S(2)}) collective-permute-start(bf16[1024,384]{1,0:T(8,128)(2,1)S(1)} %dynamic-slice_bitcast_fusion.1), channel_id=1, source_target_pairs={{0,1},{1,0},{2,3},{3,2},{4,5},{5,4},{6,7},{7,6},{8,9},{9,8},{10,11... | collective-permute-start | bytes 2359304 | tf_op jit(solution)/shard_map/ppermute | solution.py:198
  11.4 90.2 %collective-permute-start.1 = (f32[4608]{0:T(1024)S(1)}, f32[4608]{0:T(1024)S(1)}, u32[]{:S(2)}, u32[]{:S(2)}) collective-permute-start(f32[4608]{0:T(1024)S(1)} %constant_dynamic-update-slice_fusion.2), channel_id=1, source_target_pairs={{0,1},{1,0},{2,3},{3,2},{4,5},{5,4},{6,7},{7,6},{8,9},{9,8},{10,11... | collective-permute-start | bytes 55304 | tf_op jit(solution)/shard_map/ppermute | solution.py:198
  12.6 138.0 %collective-permute-start.3 = (bf16[1024,384]{1,0:T(8,128)(2,1)S(1)}, bf16[1024,384]{1,0:T(8,128)(2,1)}, u32[]{:S(2)}, u32[]{:S(2)}) collective-permute-start(bf16[1024,384]{1,0:T(8,128)(2,1)S(1)} %dynamic-slice_bitcast_fusion), channel_id=1, source_target_pairs={{0,1},{1,0},{2,3},{3,2},{4,5},{5,4},{6,7},{7,6},{8,9},{9,8},{10,11... | collective-permute-start | bytes 2359304 | tf_op jit(solution)/shard_map/ppermute | solution.py:198
  132.4 19.7 %slice-start = ((s8[4718592]{0:T(1024)(128)(4,1)}), s8[4194304]{0:T(1024)(128)(4,1)S(1)}, s32[]{:S(2)}) async-start(s8[4718592]{0:T(1024)(128)(4,1)} %bitcast.63), calls=%async_computation | async-start | bytes 8388608
  136.8 13.8 %copy-start.2 = (bf16[2,1024,384]{2,1,0:T(8,128)(2,1)S(1)}, bf16[2,1024,384]{2,1,0:T(8,128)(2,1)}, u32[]{:S(2)}) copy-start(bf16[2,1024,384]{2,1,0:T(8,128)(2,1)} %param.33) | copy-start | bytes 4718596
  136.8 15.2 %slice-start.1 = ((s8[4718592]{0:T(1024)(128)(4,1)}), s8[524288]{0:T(1024)(128)(4,1)S(1)}, s32[]{:S(2)}) async-start(s8[4718592]{0:T(1024)(128)(4,1)} %bitcast.63), calls=%async_computation.1 | async-start | bytes 1048576
  150.6 16.4 %slice-start.2 = ((s8[4718592]{0:T(1024)(128)(4,1)}), s8[4194304]{0:T(1024)(128)(4,1)S(1)}, s32[]{:S(2)}) async-start(s8[4718592]{0:T(1024)(128)(4,1)} %bitcast.68), calls=%async_computation.2 | async-start | bytes 8388608
  152.1 15.0 %slice-start.3 = ((s8[4718592]{0:T(1024)(128)(4,1)}), s8[524288]{0:T(1024)(128)(4,1)S(1)}, s32[]{:S(2)}) async-start(s8[4718592]{0:T(1024)(128)(4,1)} %bitcast.68), calls=%async_computation.3 | async-start | bytes 1048576
  167.1 9.3 %copy-start.21 = (bf16[1024,3072]{1,0:T(8,128)(2,1)S(1)}, bf16[1024,3072]{1,0:T(8,128)(2,1)}, u32[]{:S(2)}) copy-start(bf16[1024,3072]{1,0:T(8,128)(2,1)} %get-tuple-element.107) | copy-start | bytes 18874372
  184.1 9.4 %copy-start.19 = (bf16[16,48,768]{2,1,0:T(8,128)(2,1)S(1)}, bf16[16,48,768]{2,1,0:T(8,128)(2,1)}, u32[]{:S(2)}) copy-start(bf16[16,48,768]{2,1,0:T(8,128)(2,1)} %get-tuple-element.30) | copy-start | bytes 3538948
  213.5 115.1 %collective-permute-start.2 = (bf16[1024,384]{1,0:T(8,128)(2,1)}, bf16[1024,384]{1,0:T(8,128)(2,1)}, u32[]{:S(2)}, u32[]{:S(2)}) collective-permute-start(bf16[1024,384]{1,0:T(8,128)(2,1)} %constant_dynamic-slice_fusion), channel_id=1, source_target_pairs={{0,1},{1,0},{2,3},{3,2},{4,5},{5,4},{6,7},{7,6},{8,9},{9,8},{10,11... | collective-permute-start | bytes 2359304 | tf_op jit(solution)/shard_map/ppermute | solution.py:198
  (7 other events, 20.8 us)
